TPU v7x, 32 devices: a whole 2x2x4 slice. The times are simulated.
32 devices in a mesh: row: 4 (over y, x), col: 8 (over z, core).
Axes of the slice: x: 2, y: 2, z: 4, core: 2. Of those that a mesh axis runs over, the one named last changes fastest.
Arguments:
- opening_old: float32 [512, 1024], P('row', 'col'), may hold values from 0.5 to 1.5
- pressure_old: float32 [512, 1024], P('row', 'col'), may hold values from -4 to 4
- injection: float32 [512, 1024], P('row', 'col'), may hold values from 0 to 2
- front_flags: int32 [4, 512], P('row', 'col'), may hold values 0 or 1
- self_kernel: float32 [256, 256], replicated, may hold values from -0.375 to 0.375
- source_column: int32 [4, 512, 4], P('row', 'col'), may hold values from 0 to 7, all different within a row; in each aligned block of 64 rows (0 to 63, 64 to 127, ..., all dimensions but the last counted through in order) at most 64 rows name the same one
- source_tile: int32 [4, 512, 4], P('row', 'col'), may hold values from 0 to 63
- source_rank: int32 [4, 512, 4], P('row', 'col'), may hold values from 1 to 16
- left_factor: float32 [4, 512, 4, 16, 256], P('row', 'col'), may hold values from -1.5 to 1.5
- right_factor: float32 [4, 512, 4, 16, 256], P('row', 'col'), may hold values from -0.375 to 0.375
Outputs:
- opening_new: float32 [512, 1024], P('row', 'col')
- pressure_new: float32 [512, 1024], P('row', 'col')
Inputs may be any that keep to these rules, and one draw needn't show every extreme that they name: `source_column`: the 4 sources of a target tile lie in 4 different column blocks; among the 64 target tiles of one device no column block is named more than 64 times, and that count is reached.
All inputs are finite; a program needn't handle non-finite values. No bound on the sum of `front_flags` on one device may be relied on, other than what follows from the above.
Results may differ from a plain program's by a relative error of at most 0.000076.
Values sent between devices are 32-bit elements; how exact they have to be, the bound alone decides.
No kernel may reach another device: no remote copies, remote signals or barrier semaphores. Data moves between devices by JAX's collectives and lax.ppermute only.
A program may use at most 64 MiB of HBM per device.

v0:
```python
import jax
import jax.numpy as jnp
from jax import lax
from jax.sharding import PartitionSpec as P

TSIDE = 16
PASSES = 3


step_size = 0.1
highest_mode = lax.Precision.HIGHEST


def with_halo(array, sides, width):
    for axis, dim in sides:
        devices, length = (lax.axis_size(axis), array.shape[dim])
        up = [(i, (i + 1) % devices) for i in range(devices - 1)]
        down = [(j, i) for i, j in up]
        last = lax.slice_in_dim(array, length - width, length, axis=dim)
        leading = lax.slice_in_dim(array, 0, width, axis=dim)
        before = lax.ppermute(last, axis, up)
        after = lax.ppermute(leading, axis, down)
        array = jnp.concatenate([before, array, after], axis=dim)
    return array


def picard_pass(wide_open, wide_press, start_open, inject_part):
    row_count = wide_open.shape[0] - 2
    col_count = wide_open.shape[1] - 2
    cubed_open = wide_open * wide_open * wide_open

    def offset(array, shift_row, shift_col):
        return array[
            1 + shift_row : 1 + shift_row + row_count, 1 + shift_col : 1 + shift_col + col_count
        ]

    cube_middle = offset(cubed_open, 0, 0)
    press_middle = offset(wide_press, 0, 0)
    accumulated = jnp.zeros_like(cube_middle)
    for shift_row, shift_col in ((1, 0), (-1, 0), (0, 1), (0, -1)):
        conduct = (cube_middle + offset(cubed_open, shift_row, shift_col)) / 24.0
        accumulated = accumulated + conduct * (
            offset(wide_press, shift_row, shift_col) - press_middle
        )
    return start_open + step_size * (accumulated + inject_part)


def crop_margin(array, margin):
    return array[margin : array.shape[0] - margin, margin : array.shape[1] - margin]


def to_tiles(field_block):
    row_tiles = field_block.shape[0] // TSIDE
    col_tiles = field_block.shape[1] // TSIDE
    shaped = field_block.reshape(row_tiles, TSIDE, col_tiles, TSIDE).transpose(0, 2, 1, 3)
    return shaped.reshape(row_tiles * col_tiles, TSIDE * TSIDE)


def from_tiles(tile_rows, row_tiles, col_tiles):
    shaped = tile_rows.reshape(row_tiles, col_tiles, TSIDE, TSIDE).transpose(0, 2, 1, 3)
    return shaped.reshape(row_tiles * TSIDE, col_tiles * TSIDE)


def local(
    opening_old,
    pressure_old,
    injection,
    front_flags,
    self_kernel,
    source_column,
    source_tile,
    source_rank,
    left_factor,
    right_factor,
):
    block_rows, block_cols = opening_old.shape
    deep = with_halo(
        jnp.stack([opening_old, pressure_old, injection]), (("row", 1), ("col", 2)), PASSES
    )
    total_rows = block_rows * lax.axis_size("row")
    total_cols = block_cols * lax.axis_size("col")
    row_start = lax.axis_index("row") * block_rows
    col_start = lax.axis_index("col") * block_cols
    current = deep[0]
    for passes_done in range(PASSES):
        margin = PASSES - 1 - passes_done
        wide_press = crop_margin(deep[1], passes_done)
        start_open = crop_margin(deep[0], passes_done + 1)
        inject_part = crop_margin(deep[2], passes_done + 1)
        current = picard_pass(current, wide_press, start_open, inject_part)
        rows_global = row_start - margin + jnp.arange(current.shape[0], dtype=jnp.int32)
        cols_global = col_start - margin + jnp.arange(current.shape[1], dtype=jnp.int32)
        row_inside = (rows_global >= 0) & (rows_global < total_rows)
        col_inside = (cols_global >= 0) & (cols_global < total_cols)
        current = jnp.where(row_inside[:, None] & col_inside[None, :], current, 0.0)
    row_tiles = block_rows // TSIDE
    col_tiles = block_cols // TSIDE
    tile_rows = to_tiles(current) * front_flags[0][:, None].astype(jnp.float32)
    opening_new = from_tiles(tile_rows, row_tiles, col_tiles)
    tile_count = tile_rows.shape[0]
    links = source_column.shape[2]
    columns = source_column[0].reshape(-1)
    picks = source_tile[0].reshape(-1)
    band = lax.all_gather(tile_rows, "col", axis=0, tiled=True)
    sources = band[columns * tile_count + picks]
    sources = sources.reshape(tile_count, links, -1)
    rank_keep = (
        jnp.arange(right_factor.shape[3], dtype=jnp.int32)[None, None, :]
        < source_rank[0][:, :, None]
    ).astype(jnp.float32)
    coefficients = (
        jnp.einsum("tkjs,tks->tkj", right_factor[0], sources, precision=highest_mode) * rank_keep
    )
    near_terms = jnp.einsum("tkjs,tkj->ts", left_factor[0], coefficients, precision=highest_mode)
    self_terms = jnp.einsum("su,tu->ts", self_kernel, tile_rows, precision=highest_mode)
    pressure_new = from_tiles(self_terms + near_terms, row_tiles, col_tiles)
    return (opening_new, pressure_new)


def solution(mesh):
    return jax.shard_map(
        local,
        mesh=mesh,
        in_specs=(
            P("row", "col"),
            P("row", "col"),
            P("row", "col"),
            P("row", "col"),
            P(),
            P("row", "col", None),
            P("row", "col", None),
            P("row", "col", None),
            P("row", "col", None, None, None),
            P("row", "col", None, None, None),
        ),
        out_specs=(P("row", "col"), P("row", "col")),
        check_vma=False,
    )
```

profile of v0, /device:TPU:0, one launch (start us, length us, event | category | flops | bytes accessed | tf_op | source)
XLA Modules:
  0.0 51.3 jit_solution(16274650812509048601)
XLA Ops:
  0.6 0.8 %pad_maximum_fusion.4 = (f32[3,3,128]{2,1,0:T(4,128)S(1)}, f32[3,3,128]{2,1,0:T(4,128)S(1)}) fusion(f32[1,128,128]{2,1,0:T(8,128)} %bitcast.44, f32[1,128,128]{2,1,0:T(8,128)} %bitcast.47, f32[1,128,128]{2,1,0:T(8,128)} %bitcast.50), kind=kLoop, calls=%fused_computation.89 | loop fusion | flops 4608 | bytes 205824 | tf_op jit(solution)/shard_map/slice | solution.py:19
  1.5 1.3 %collective-permute-start.1 = (f32[3,3,128]{2,1,0:T(4,128)S(1)}, f32[3,3,128]{2,1,0:T(4,128)S(1)}, u32[]{:S(2)}, u32[]{:S(2)}) collective-permute-start(f32[3,3,128]{2,1,0:T(4,128)S(1)} %get-tuple-element.10), channel_id=1, source_target_pairs={{8,0},{16,8},{24,16},{9,1},{17,9},{25,17},{10,2},{18,10},{26,18},{... | collective-permute-start | bytes 13832 | tf_op jit(solution)/shard_map/ppermute | solution.py:22
  2.7 5.5 %collective-permute-start = (f32[3,3,128]{2,1,0:T(4,128)S(1)}, f32[3,3,128]{2,1,0:T(4,128)S(1)}, u32[]{:S(2)}, u32[]{:S(2)}) collective-permute-start(f32[3,3,128]{2,1,0:T(4,128)S(1)} %get-tuple-element.9), channel_id=1, source_target_pairs={{0,8},{8,16},{16,24},{1,9},{9,17},{17,25},{2,10},{10,18},{18,26},{... | collective-permute-start | bytes 13832 | tf_op jit(solution)/shard_map/ppermute | solution.py:21
  8.3 0.7 %convert_reduce_fusion = f32[64]{0:T(128)S(1)} fusion(s32[1,64]{1,0:T(1,128)} %param.13), kind=kLoop, calls=%fused_computation.100 | loop fusion | flops 64 | bytes 512 | tf_op jit(solution)/shard_map/convert_element_type | solution.py:98
  9.0 0.7 %convert_bitcast_fusion = f32[64]{0:T(128)S(1)} fusion(s32[1,64]{1,0:T(1,128)} %param.13), kind=kLoop, calls=%fused_computation.99 | loop fusion | flops 64 | bytes 512 | tf_op jit(solution)/shard_map/convert_element_type | solution.py:98
  9.6 0.7 %multiply_add_fusion = s32[1,64,4]{1,2,0:T(4,128)S(1)} fusion(s32[1,64,4]{1,2,0:T(4,128)} %param.16, s32[1,64,4]{1,2,0:T(4,128)} %param.15), kind=kLoop, calls=%fused_computation.92 | loop fusion | flops 512 | bytes 3072 | tf_op jit(solution)/shard_map/add | solution.py:105
  10.3 0.1 copy.17
  10.4 0.1 add.214
  10.6 0.9 %pad_maximum_fusion.1 = f32[3,134,128]{2,1,0:T(8,128)S(1)} fusion(f32[3,3,128]{2,1,0:T(4,128)S(1)} %collective-permute-done.1, f32[1,128,128]{2,1,0:T(8,128)} %bitcast.45, f32[1,128,128]{2,1,0:T(8,128)} %bitcast.48, f32[1,128,128]{2,1,0:T(8,128)} %bitcast.51, f32[3,3,128]{2,1,0:T(4,128)S(1)} %collective-permute-done), kind=kLoop, calls=%fused_computation.8 | loop fusion | flops 205824 | bytes 411648 | tf_op jit(solution)/shard_map/concatenate | solution.py:23
  11.5 0.1 fusion.49
  11.6 1.3 %collective-permute-start.3 = (f32[3,134,3]{2,1,0:T(8,128)S(1)}, f32[3,134,3]{2,1,0:T(8,128)S(1)}, u32[]{:S(2)}, u32[]{:S(2)}) collective-permute-start(f32[3,134,3]{2,1,0:T(8,128)S(1)} %get-tuple-element.8), channel_id=1, source_target_pairs={{1,0},{2,1},{3,2},{4,3},{5,4},{6,5},{7,6},{9,8},{10,9},{11,10},{12... | collective-permute-start | bytes 14480 | tf_op jit(solution)/shard_map/ppermute | solution.py:22
  12.9 3.0 %collective-permute-start.2 = (f32[3,134,3]{2,1,0:T(8,128)S(1)}, f32[3,134,3]{2,1,0:T(8,128)S(1)}, u32[]{:S(2)}, u32[]{:S(2)}) collective-permute-start(f32[3,134,3]{2,1,0:T(8,128)S(1)} %get-tuple-element.7), channel_id=1, source_target_pairs={{0,1},{1,2},{2,3},{3,4},{4,5},{5,6},{6,7},{8,9},{9,10},{10,11},{11... | collective-permute-start | bytes 14480 | tf_op jit(solution)/shard_map/ppermute | solution.py:21
  16.1 0.1 mul.138
  16.2 0.2 mul.139
  16.4 0.8 %copy.16 = s32[64,4]{1,0:T(8,128)S(1)} copy(s32[64,4]{0,1:T(4,128)} %bitcast.56) | data formatting | bytes 2048 | tf_op jit(solution)/shard_map/lt | solution.py:108
  17.2 1.2 %pad_maximum_fusion = f32[3,134,134]{2,1,0:T(8,128)S(1)} fusion(f32[3,134,3]{2,1,0:T(8,128)S(1)} %collective-permute-done.3, f32[3,3,128]{2,1,0:T(4,128)S(1)} %collective-permute-done.1, f32[1,128,128]{2,1,0:T(8,128)} %bitcast.46, f32[1,128,128]{2,1,0:T(8,128)} %bitcast.49, f32[1,128,128]{2,1,0:T(8,128)} %bitcast.52, ...), kind=kLoop, calls=%fused_computation.7 | loop fusion | flops 323208 | bytes 430944 | tf_op jit(solution)/shard_map/concatenate | solution.py:23
  18.4 0.5 multiply_multiply_fusion.1
  18.9 0.5 multiply_multiply_fusion
  19.3 0.9 %fusion.47 = (f32[128,128]{1,0:T(8,128)}, f32[128,128]{1,0:T(8,128)S(1)}) fusion(f32[128,128]{1,0:T(8,128)S(1)} %mul.139, f32[134,134]{1,0:T(8,128)S(1)} %get-tuple-element.5, f32[134,134]{1,0:T(8,128)S(1)} %get-tuple-element.6, f32[130,130]{1,0:T(8,128)S(1)} %multiply_multiply_fusion, f32[134,134]{1,0:T(8,128)S(1)} %get-tuple-element.4, ...), kind=kLoop, calls=%fused_computation.101 | loop fusion | flops 409600 | bytes 983296 | tf_op jit(solution)/shard_map/mul | solution.py:98
  20.3 0.2 reshape.112
  20.4 0.1 copy.25
  20.5 0.2 reshape.113
  20.9 19.2 %all_gather.3 = f32[512,256]{1,0:T(8,128)S(1)} all-gather(f32[64,256]{1,0:T(8,128)S(1)} %broadcast_multiply_fusion), channel_id=1, replica_groups=mesh['row'=4,'col'=8] {'col'}, dimensions={0}, use_global_device_ids=true | all-gather | bytes 589824 | tf_op jit(solution)/shard_map/all_gather | solution.py:104
  40.1 1.0 %gather_fusion = f32[256,256]{1,0:T(8,128)S(1)} fusion(f32[512,256]{1,0:T(8,128)S(1)} %all_gather.3, s32[1024]{0:T(1024)S(1)} %pad_clamp_fusion), kind=kCustom, calls=%fused_computation | custom fusion | bytes 525312 | tf_op jit(solution)/shard_map/gather | solution.py:105
  41.1 0.3 reshape.130
  41.3 5.9 %fusion.2 = f32[64,4,1,16]{3,2,1,0:T(1,128)S(1)} fusion(f32[64,4,256,1]{2,3,1,0:T(1,128)S(1)} %reshape.130, f32[1,64,4,16,256]{4,3,2,1,0:T(8,128)} %param.19), kind=kOutput, calls=%fused_computation.3 | convolution fusion | flops 12582912 | bytes 4472832 | tf_op jit(solution)/shard_map/tkjs,tks->tkj/dot_general | solution.py:112
  47.2 0.1 fusion.32
  47.4 2.4 %fusion = f32[64,1,256,1]{2,1,3,0:T(1,128)S(1)} fusion(f32[64,4,16,1]{2,3,1,0:T(1,128)S(1)} %bitcast.54, f32[1,64,4,16,256]{4,3,2,1,0:T(8,128)S(1)} %copy-done.1), kind=kOutput, calls=%fused_computation.1 | convolution fusion | flops 12582912 | bytes 4276224 | tf_op jit(solution)/shard_map/tkjs,tkj->ts/dot_general | solution.py:114
  49.7 0.4 convolution_add_fusion
  50.1 0.2 reshape.115
  50.3 0.2 copy.18
  50.5 0.8 %reshape.116 = f32[128,128]{1,0:T(8,128)} reshape(f32[8,16,8,16]{3,2,1,0:T(8,128)S(1)} %copy.18) | data formatting | bytes 131072 | tf_op jit(solution)/shard_map/reshape | solution.py:61
  (17 shorter events, 0.3 us)
Async XLA Ops:
  0.6 49.1 %copy-start = (f32[256,256]{1,0:T(8,128)S(1)}, f32[256,256]{1,0:T(8,128)}, u32[]{:S(2)}) copy-start(f32[256,256]{1,0:T(8,128)} %param.14) | copy-start | bytes 786436
  1.5 9.1 %collective-permute-start.1 = (f32[3,3,128]{2,1,0:T(4,128)S(1)}, f32[3,3,128]{2,1,0:T(4,128)S(1)}, u32[]{:S(2)}, u32[]{:S(2)}) collective-permute-start(f32[3,3,128]{2,1,0:T(4,128)S(1)} %get-tuple-element.10), channel_id=1, source_target_pairs={{8,0},{16,8},{24,16},{9,1},{17,9},{25,17},{10,2},{18,10},{26,18},{... | collective-permute-start | bytes 13832 | tf_op jit(solution)/shard_map/ppermute | solution.py:22
  2.7 7.8 %collective-permute-start = (f32[3,3,128]{2,1,0:T(4,128)S(1)}, f32[3,3,128]{2,1,0:T(4,128)S(1)}, u32[]{:S(2)}, u32[]{:S(2)}) collective-permute-start(f32[3,3,128]{2,1,0:T(4,128)S(1)} %get-tuple-element.9), channel_id=1, source_target_pairs={{0,8},{8,16},{16,24},{1,9},{9,17},{17,25},{2,10},{10,18},{18,26},{... | collective-permute-start | bytes 13832 | tf_op jit(solution)/shard_map/ppermute | solution.py:21
  11.6 5.5 %collective-permute-start.3 = (f32[3,134,3]{2,1,0:T(8,128)S(1)}, f32[3,134,3]{2,1,0:T(8,128)S(1)}, u32[]{:S(2)}, u32[]{:S(2)}) collective-permute-start(f32[3,134,3]{2,1,0:T(8,128)S(1)} %get-tuple-element.8), channel_id=1, source_target_pairs={{1,0},{2,1},{3,2},{4,3},{5,4},{6,5},{7,6},{9,8},{10,9},{11,10},{12... | collective-permute-start | bytes 14480 | tf_op jit(solution)/shard_map/ppermute | solution.py:22
  12.9 4.2 %collective-permute-start.2 = (f32[3,134,3]{2,1,0:T(8,128)S(1)}, f32[3,134,3]{2,1,0:T(8,128)S(1)}, u32[]{:S(2)}, u32[]{:S(2)}) collective-permute-start(f32[3,134,3]{2,1,0:T(8,128)S(1)} %get-tuple-element.7), channel_id=1, source_target_pairs={{0,1},{1,2},{2,3},{3,4},{4,5},{5,6},{6,7},{8,9},{9,10},{10,11},{11... | collective-permute-start | bytes 14480 | tf_op jit(solution)/shard_map/ppermute | solution.py:21
  41.3 6.0 %copy-start.1 = (f32[1,64,4,16,256]{4,3,2,1,0:T(8,128)S(1)}, f32[1,64,4,16,256]{4,3,2,1,0:T(8,128)}, u32[]{:S(2)}) copy-start(f32[1,64,4,16,256]{4,3,2,1,0:T(8,128)} %param.18) | copy-start | bytes 12582916
where the time goes:
time: 52.3 us; the launch traced here: 51.3 us
  blocking collectives  19.2 us (37%)
  starting transfers between devices  11.1 us (21%)
  matrix products  8.59 us (16%)
  other arithmetic  7.04 us (13%)
  local copies, waits for them, and re-layouts  4.42 us (8%)
  between operations  0.87 us (2%)
    all_gather x1, blocking collectives, local(): band = lax.all_gather(tile_rows, 'col', axis=0, tiled=True)  19.2 us
    ppermute x2, starting transfers between devices, with_halo(): before = lax.ppermute(last, axis, up)  8.54 us
    dot_general x1, matrix products, local(): jnp.einsum('tkjs,tks->tkj', right_factor[0], sources, precision=highest_m...  5.86 us
    ppermute x2, starting transfers between devices, with_halo(): after = lax.ppermute(leading, axis, down)  2.57 us
    dot_general x1, matrix products, local(): jnp.einsum('tkjs,tkj->ts', left_factor[0], coefficients, precision=highes...  2.35 us
    concatenate x2, other arithmetic, with_halo(): array = jnp.concatenate([before, array, after], axis=dim)  2.08 us
    convert_element_type x2, other arithmetic, local(): tile_rows = to_tiles(current) * front_flags[0][:, None].astype(jnp.float32)  1.33 us
  transfers between devices with their start and end apart: 4, of which 0 were waited for; matrix products, arithmetic and copies ran while one was open for 7% of the time, Pallas kernels for 0%

commit v1 on v0

v1 whole, which is shorter than its diff:
```python
import functools

import jax
import jax.numpy as jnp
from jax import lax
from jax.experimental import pallas as pl
from jax.experimental.pallas import tpu as pltpu
from jax.sharding import PartitionSpec as P

TSIDE = 16
PASSES = 3
LANES = 128
SUB = 8
step_size = 0.1


def neighbour_pairs(count, first):
    pairs = [(i, i) for i in range(count)]
    for i in range(first, count - 1, 2):
        pairs[i], pairs[i + 1] = (i, i + 1), (i + 1, i)
    return pairs


def iota(shape, axis):
    return lax.broadcasted_iota(jnp.int32, shape, axis)


def edges_kernel(open_ref, press_ref, inject_ref, rows_ref, cols_ref):
    sub = iota((SUB, LANES), 0)
    lane = iota((SUB, LANES), 1)
    rows = open_ref.shape[0]
    for f, ref in enumerate((open_ref, press_ref, inject_ref)):
        rows_ref[f * SUB : (f + 1) * SUB, :] = jnp.where(
            sub < SUB // 2, ref[0:SUB, :], ref[rows - SUB : rows, :]
        )
        packed = jnp.zeros((SUB, LANES), jnp.float32)
        for g in range(rows // SUB):
            moved = pltpu.roll(ref[g * SUB : (g + 1) * SUB, :], (3 + 8 * g) % LANES, 1)
            packed = jnp.where(lane // 8 == g, moved, packed)
        cols_ref[f * SUB : (f + 1) * SUB, :] = packed


def swap_groups(value):
    sub = iota(value.shape, value.ndim - 2)
    group = iota(value.shape, value.ndim - 1) // TSIDE
    row_axis, lane_axis = value.ndim - 2, value.ndim - 1
    for d in (1, 2, 4):
        low_row, low_group = (sub & d) == 0, (group & d) == 0
        up = pltpu.roll(pltpu.roll(value, SUB - d, row_axis), TSIDE * d, lane_axis)
        down = pltpu.roll(pltpu.roll(value, d, row_axis), LANES - TSIDE * d, lane_axis)
        value = jnp.where(
            low_row == low_group, value, jnp.where(low_row, up, down)
        )
    return value


def picard(opening, pressure, inject, inside):
    rows, cols = opening.shape[-2:]
    row_axis, col_axis = opening.ndim - 2, opening.ndim - 1
    shifts = ((row_axis, rows - 1), (row_axis, 1), (col_axis, cols - 1), (col_axis, 1))
    pressure = jnp.where(inside, pressure, 0.0)
    opening = jnp.where(inside, opening, 0.0)
    base = jnp.where(inside, opening + step_size * inject, 0.0)
    slopes = [
        jnp.where(inside, (pltpu.roll(pressure, s, a) - pressure) * (step_size / 24.0), 0.0)
        for a, s in shifts
    ]
    current = opening
    for _ in range(PASSES):
        cubed = current * current * current
        current = base
        for (a, s), slope in zip(shifts, slopes):
            current = current + (cubed + pltpu.roll(cubed, s, a)) * slope
    return current


def stencil_kernel(
    counts,
    flag_ref,
    flags_ref,
    open_ref,
    press_ref,
    inject_ref,
    rows_a_ref,
    rows_b_ref,
    cols_a_ref,
    cols_b_ref,
    out_ref,
):
    n_row, n_col = counts
    rows, cols = open_ref.shape
    wide, tall = cols + LANES, rows + SUB
    me_row, me_col = lax.axis_index("row"), lax.axis_index("col")
    row_even, col_even = me_row % 2 == 0, me_col % 2 == 0
    sub = iota((SUB, LANES), 0)
    lane = iota((SUB, LANES), 1)
    fields, tails = [], []
    for f, ref in enumerate((open_ref, press_ref, inject_ref)):
        part = slice(f * SUB, (f + 1) * SUB)
        below = jnp.where(row_even, rows_a_ref[part, :], rows_b_ref[part, :])
        above = jnp.where(row_even, rows_b_ref[part, :], rows_a_ref[part, :])
        tail = jnp.where(sub < SUB // 2, below, above)
        right = jnp.where(col_even, cols_a_ref[part, :], cols_b_ref[part, :])
        left = jnp.where(col_even, cols_b_ref[part, :], cols_a_ref[part, :])
        packed = jnp.where(lane % 8 < 3, left, right)
        sides = []
        for g in range(rows // SUB):
            moved = pltpu.roll(packed, (LANES - 3 - 8 * g) % LANES, 1)
            sides.append(jnp.where((lane < 3) | (lane >= LANES - 3), moved, 0.0))
        sides.append(jnp.zeros((SUB, LANES), jnp.float32))
        main = jnp.concatenate([ref[...], tail], axis=0)
        fields.append(jnp.concatenate([main, jnp.concatenate(sides, axis=0)], axis=1))
        tails.append(tail)
    row = iota((tall, wide), 0)
    col = iota((tall, wide), 1)
    row = me_row * rows + jnp.where(row < rows + SUB // 2, row, row - tall)
    col = me_col * cols + jnp.where(col < cols + LANES // 2, col, col - wide)
    inside = (row >= 0) & (row < n_row * rows) & (col >= 0) & (col < n_col * cols)
    current = picard(*fields, inside)[:rows, :cols]
    tiles = swap_groups(current.reshape(rows // SUB, SUB, LANES))
    count = flags_ref.shape[1]
    ones = jnp.where(iota((count, count), 0) == iota((count, count), 1), flags_ref[...], 0)
    flags = jnp.sum(ones.astype(jnp.float32), axis=1, keepdims=True)
    for a in range(rows // TSIDE):
        for h in range(2):
            out_ref[a * 8 : a * 8 + 8, h * LANES : (h + 1) * LANES] = (
                tiles[2 * a + h] * flags[a * 8 : a * 8 + 8, :]
            )
    corner = jnp.zeros((SUB, LANES), jnp.float32)
    for f, ref in enumerate((open_ref, press_ref, inject_ref)):
        top = pltpu.roll(jnp.where(sub < 5, ref[0:SUB, :], tails[f]), 3, 0)
        bottom = pltpu.roll(jnp.where(sub >= 3, ref[rows - SUB : rows, :], tails[f]), 5, 0)
        for b, window in enumerate((top, bottom)):
            at = (f * 2 + b) * 10
            corner = jnp.where(
                (lane >= at + 5) & (lane < at + 10), pltpu.roll(window, at + 5, 1), corner
            )
            corner = jnp.where(
                (lane >= 64 + at) & (lane < 69 + at),
                pltpu.roll(window, (64 + at - (LANES - 5)) % LANES, 1),
                corner,
            )
    out_ref[count : count + SUB, 0:LANES] = corner
    side = cols // TSIDE
    marks = jnp.zeros((SUB, LANES), jnp.float32)
    for at, tile in ((0, 0), (10, count - side), (64, side - 1), (74, count - 1)):
        marks = jnp.where(
            (lane >= at) & (lane < at + 10), flag_ref[0, tile].astype(jnp.float32), marks
        )
    out_ref[count : count + SUB, LANES : 2 * LANES] = marks


def split_dot(left, right):
    dims = (((1,), (1,)), ((), ()))

    def dot(a, b):
        return lax.dot_general(a, b, dims, preferred_element_type=jnp.float32)

    left_high = left.astype(jnp.bfloat16)
    left_low = (left - left_high.astype(jnp.float32)).astype(jnp.bfloat16)
    right_high = right.astype(jnp.bfloat16)
    right_low = (right - right_high.astype(jnp.float32)).astype(jnp.bfloat16)
    return dot(left_high, right_high) + (dot(left_high, right_low) + dot(left_low, right_high))


def pressure_kernel(
    counts,
    column_ref,
    tile_ref,
    rank_ref,
    near_ref,
    far_ref,
    self_ref,
    right_ref,
    left_ref,
    open_out,
    press_out,
    band,
    press,
    fixes,
):
    n_row, n_col = counts
    me_row, me_col = lax.axis_index("row"), lax.axis_index("col")
    count = press.shape[0]
    block = count + SUB
    half = near_ref.shape[0]
    rows, cols = open_out.shape
    side = cols // TSIDE
    sub = iota((SUB, LANES), 0)
    lane = iota((SUB, LANES), 1)
    for h in range(2):
        part = slice(h * LANES, (h + 1) * LANES)
        band[h, 0:half, :] = near_ref[:, part]
        band[h, half : 2 * half, :] = far_ref[:, part]

    def place(column):
        step = column ^ me_col
        return ((step >> 1) + (step & 1) * (n_col // 2)) * block

    starts = [place(c) for c in range(n_col)]
    starts = [pl.multiple_of(s, SUB) for s in starts]
    corners = [[band[h, pl.ds(s + count, SUB), :] for h in range(2)] for s in starts]
    outside = ((sub < 3) & (lane < 10) & (me_row == 0)) | (
        (sub >= 5) & (lane >= 10) & (me_row == n_row - 1)
    )
    left_part = (lane % 10) < 5
    for c in range(n_col - 1):
        a, b = corners[c], corners[c + 1]
        window, marks = (jnp.where(left_part, pltpu.roll(x, 64, 1), y) for x, y in zip(a, b))
        fixed = picard(
            window,
            pltpu.roll(window, LANES - 20, 1),
            pltpu.roll(window, LANES - 40, 1),
            jnp.logical_not(outside),
        )
        fixes[c * SUB : (c + 1) * SUB, :] = fixed * marks
    row_lane = iota((1, LANES), 1)
    for c in range(n_col - 1):
        third = fixes[c * SUB + 3 : c * SUB + 4, :]
        fourth = fixes[c * SUB + 4 : c * SUB + 5, :]
        for start, tile, part, long_row, short_row, long_at, short_at, source in (
            (starts[c], side - 1, 0, third, fourth, (14, 16), (31, 32), (3, 4)),
            (starts[c + 1], 0, 0, third, fourth, (0, 2), (16, 17), (5, 5)),
            (starts[c], count - 1, 1, fourth, third, (126, 128), (111, 112), (13, 14)),
            (starts[c + 1], count - side, 1, fourth, third, (112, 114), (96, 97), (15, 15)),
        ):
            spot = (part, pl.ds(start + tile, 1), slice(None))
            value = band[spot]
            value = jnp.where(
                (row_lane >= long_at[0]) & (row_lane < long_at[1]),
                pltpu.roll(long_row, (long_at[0] - source[0]) % LANES, 1),
                value,
            )
            value = jnp.where(
                row_lane == short_at[0],
                pltpu.roll(short_row, (short_at[0] - source[1]) % LANES, 1),
                value,
            )
            band[spot] = value

    links, ranks = right_ref.shape[1], right_ref.shape[2]
    depth = iota((ranks, LANES), 0)

    def target(t, carry):
        total = jnp.zeros((ranks, 2 * LANES), jnp.float32)
        for k in range(links):
            at = place(column_ref[k, t]) + tile_ref[k, t]
            product = sum(
                right_ref[t, k, :, h * LANES : (h + 1) * LANES] * band[h, pl.ds(at, 1), :]
                for h in range(2)
            )
            coefficient = jnp.sum(product, axis=1, keepdims=True)
            coefficient = jnp.where(depth < rank_ref[k, t], coefficient, 0.0)
            total = total + left_ref[t, k] * jnp.concatenate([coefficient, coefficient], axis=1)
        press[pl.ds(t, 1), :] = jnp.sum(total, axis=0, keepdims=True)
        return carry

    lax.fori_loop(0, count, target, 0, unroll=4)
    own = jnp.concatenate([band[0, 0:count, :], band[1, 0:count, :]], axis=1)
    result = press[...] + split_dot(own, self_ref[...])

    def lay_out(tiles):
        parts = [
            tiles[8 * a : 8 * a + 8, h * LANES : (h + 1) * LANES]
            for a in range(rows // TSIDE)
            for h in range(2)
        ]
        return swap_groups(jnp.stack(parts)).reshape(rows, cols)

    open_out[...] = lay_out(own)
    press_out[...] = lay_out(result)


def local(
    opening_old,
    pressure_old,
    injection,
    front_flags,
    self_kernel,
    source_column,
    source_tile,
    source_rank,
    left_factor,
    right_factor,
):
    n_row, n_col = lax.axis_size("row"), lax.axis_size("col")
    counts = (n_row, n_col)
    rows, cols = opening_old.shape
    count = front_flags.shape[1]
    links = source_column.shape[2]
    vmem = pl.BlockSpec(memory_space=pltpu.VMEM)
    smem = pl.BlockSpec(memory_space=pltpu.SMEM)
    f32 = jnp.float32
    edge_rows, edge_cols = pl.pallas_call(
        edges_kernel,
        out_shape=[jax.ShapeDtypeStruct((3 * SUB, LANES), f32)] * 2,
        in_specs=[vmem] * 3,
        out_specs=[vmem] * 2,
    )(opening_old, pressure_old, injection)
    rows_b = lax.ppermute(edge_rows, "row", neighbour_pairs(n_row, 1))
    rows_a = lax.ppermute(edge_rows, "row", neighbour_pairs(n_row, 0))
    cols_b = lax.ppermute(edge_cols, "col", neighbour_pairs(n_col, 1))
    cols_a = lax.ppermute(edge_cols, "col", neighbour_pairs(n_col, 0))
    block = pl.pallas_call(
        functools.partial(stencil_kernel, counts),
        out_shape=jax.ShapeDtypeStruct((count + SUB, 2 * LANES), f32),
        in_specs=[smem] + [vmem] * 8,
        out_specs=vmem,
    )(
        front_flags,
        front_flags,
        opening_old,
        pressure_old,
        injection,
        rows_a,
        rows_b,
        cols_a,
        cols_b,
    )

    def exchange(value, step):
        return lax.ppermute(value, "col", [(i, i ^ step) for i in range(n_col)])

    near = jnp.concatenate([block] + [exchange(block, s) for s in range(2, n_col, 2)], axis=0)
    far = exchange(near, 1)
    opening_new, pressure_new = pl.pallas_call(
        functools.partial(pressure_kernel, counts),
        out_shape=[jax.ShapeDtypeStruct((rows, cols), f32)] * 2,
        in_specs=[smem] * 3 + [vmem] * 5,
        out_specs=[vmem] * 2,
        scratch_shapes=[
            pltpu.VMEM((2, n_col * (count + SUB), LANES), f32),
            pltpu.VMEM((count, 2 * LANES), f32),
            pltpu.VMEM((n_col * SUB, LANES), f32),
        ],
    )(
        source_column[0].T,
        source_tile[0].T,
        source_rank[0].T,
        near,
        far,
        self_kernel,
        right_factor[0],
        left_factor[0],
    )
    return opening_new, pressure_new


def solution(mesh):
    return jax.shard_map(
        local,
        mesh=mesh,
        in_specs=(
            P("row", "col"),
            P("row", "col"),
            P("row", "col"),
            P("row", "col"),
            P(),
            P("row", "col", None),
            P("row", "col", None),
            P("row", "col", None),
            P("row", "col", None, None, None),
            P("row", "col", None, None, None),
        ),
        out_specs=(P("row", "col"), P("row", "col")),
        check_vma=False,
    )
```

time: 52.3 us -> 39.3 us (0.75); the launches traced: 51.3 us -> 38.9 us
  blocking collectives: 19.2 us -> 0 us
  Pallas kernels: 0 us -> 11.9 us
  waiting for transfers between devices: 0.01 us -> 8.66 us
  matrix products: 8.59 us -> 0 us
  other arithmetic: 7.04 us -> 0.91 us
  starting transfers between devices: 11.1 us -> 15.4 us
  local copies, waits for them, and re-layouts: 4.42 us -> 1.32 us
    all_gather x1 -> x0, blocking collectives: 19.2 us -> none  [local(): band = lax.all_gather(tile_rows, 'col', axis=0, tiled=True)]
    pallas_call x0 -> x3, Pallas kernels: none -> 11.9 us  [the longest x1 7.87 us: local(): pl.pallas_call(functools.partial(pressure_kernel, counts), out_shape=[jax...]
    ppermute x4 -> x8, waiting for transfers between devices: 0.01 us -> 8.66 us  [the longest x4 7.65 us: exchange(): return lax.ppermute(value, 'col', [(i, i ^ step) for i in range(n_col)])]
    dot_general x3 -> x0, matrix products: 8.59 us -> none  [the longest x1 5.86 us: local(): jnp.einsum('tkjs,tks->tkj', right_factor[0], sources, precision=highest_m...]
    ppermute x4 -> x8, starting transfers between devices: 11.1 us -> 15.4 us  [the longest x4 5.33 us: exchange(): return lax.ppermute(value, 'col', [(i, i ^ step) for i in range(n_col)])]
    mul x6 -> x0, other arithmetic: 2.08 us -> none  [the longest x2 0.98 us: local(): tile_rows = to_tiles(current) * front_flags[0][:, None].astype(jnp.float32)]
    reshape x6 -> x0, local copies, waits for them, and re-layouts: 1.79 us -> none  [the longest x1 0.82 us: from_tiles(): return shaped.reshape(row_tiles * TSIDE, col_tiles * TSIDE)]
    convert_element_type x2 -> x0, other arithmetic: 1.33 us -> none  [local(): tile_rows = to_tiles(current) * front_flags[0][:, None].astype(jnp.float32)]
  transfers between devices with their start and end apart: 4 -> 8, of which waited for: 0 -> 4; matrix products, arithmetic and copies ran while one was open for 7% -> 0% of each run, Pallas kernels for 0% -> 0%
where the time goes in v1:
time: 39.3 us; the launch traced here: 38.9 us
  starting transfers between devices  15.4 us (39%)
  Pallas kernels  11.9 us (30%)
  waiting for transfers between devices  8.66 us (22%)
  local copies, waits for them, and re-layouts  1.32 us (3%)
  other arithmetic  0.91 us (2%)
  between operations  0.69 us (2%)
    pallas_call x1, Pallas kernels, local(): pl.pallas_call(functools.partial(pressure_kernel, counts), out_shape=[jax...  7.87 us
    ppermute x4, waiting for transfers between devices, exchange(): return lax.ppermute(value, 'col', [(i, i ^ step) for i in range(n_col)])  7.65 us
    ppermute x4, starting transfers between devices, exchange(): return lax.ppermute(value, 'col', [(i, i ^ step) for i in range(n_col)])  5.33 us
    ppermute x1, starting transfers between devices, local(): rows_a = lax.ppermute(edge_rows, 'row', neighbour_pairs(n_row, 0))  5.07 us
    pallas_call x1, Pallas kernels, local(): pl.pallas_call(functools.partial(stencil_kernel, counts), out_shape=jax.S...  2.4 us
    ppermute x1, starting transfers between devices, local(): cols_a = lax.ppermute(edge_cols, 'col', neighbour_pairs(n_col, 0))  2.31 us
    pallas_call x1, Pallas kernels, local(): pl.pallas_call(edges_kernel, out_shape=[jax.ShapeDtypeStruct((3 * SUB, LA...  1.62 us
    ppermute x1, starting transfers between devices, local(): rows_b = lax.ppermute(edge_rows, 'row', neighbour_pairs(n_row, 1))  1.35 us
  transfers between devices with their start and end apart: 8, of which 4 were waited for; matrix products, arithmetic and copies ran while one was open for 0% of the time, Pallas kernels for 0%

profile of v1, /device:TPU:0, one launch (start us, length us, event | category | flops | bytes accessed | tf_op | source)
XLA Modules:
  0.0 38.9 jit_solution(13130224972273279726)
XLA Ops:
  0.6 1.6 %shard_map.113 = (f32[24,128]{1,0:T(8,128)}, f32[24,128]{1,0:T(8,128)}) custom-call(f32[128,128]{1,0:T(8,128)} %open_ref.3, f32[128,128]{1,0:T(8,128)} %press_ref.3, f32[128,128]{1,0:T(8,128)} %inject_ref.3), custom_call_target="tpu_custom_call" | custom-call | tf_op jit(solution)/shard_map/pallas_call | solution.py:294
  2.3 1.4 %collective-permute-start.1 = (f32[24,128]{1,0:T(8,128)}, f32[24,128]{1,0:T(8,128)S(1)}, u32[]{:S(2)}, u32[]{:S(2)}) collective-permute-start(f32[24,128]{1,0:T(8,128)} %get-tuple-element.4), channel_id=1, source_target_pairs={{0,0},{8,16},{16,8},{24,24},{1,1},{9,17},{17,9},{25,25},{2,2},{10,... | collective-permute-start | bytes 36872 | tf_op jit(solution)/shard_map/ppermute | solution.py:300
  3.6 5.1 %collective-permute-start = (f32[24,128]{1,0:T(8,128)}, f32[24,128]{1,0:T(8,128)S(1)}, u32[]{:S(2)}, u32[]{:S(2)}) collective-permute-start(f32[24,128]{1,0:T(8,128)} %get-tuple-element.4), channel_id=1, source_target_pairs={{0,8},{8,0},{16,24},{24,16},{1,9},{9,1},{17,25},{25,17},{2,10},{10... | collective-permute-start | bytes 36872 | tf_op jit(solution)/shard_map/ppermute | solution.py:301
  8.7 1.4 %collective-permute-start.3 = (f32[24,128]{1,0:T(8,128)}, f32[24,128]{1,0:T(8,128)S(1)}, u32[]{:S(2)}, u32[]{:S(2)}) collective-permute-start(f32[24,128]{1,0:T(8,128)} %get-tuple-element.5), channel_id=1, source_target_pairs={{0,0},{1,2},{2,1},{3,4},{4,3},{5,6},{6,5},{7,7},{8,8},{9,10},{10,9... | collective-permute-start | bytes 36872 | tf_op jit(solution)/shard_map/ppermute | solution.py:302
  10.0 2.3 %collective-permute-start.2 = (f32[24,128]{1,0:T(8,128)}, f32[24,128]{1,0:T(8,128)S(1)}, u32[]{:S(2)}, u32[]{:S(2)}) collective-permute-start(f32[24,128]{1,0:T(8,128)} %get-tuple-element.5), channel_id=1, source_target_pairs={{0,1},{1,0},{2,3},{3,2},{4,5},{5,4},{6,7},{7,6},{8,9},{9,8},{10,11... | collective-permute-start | bytes 36872 | tf_op jit(solution)/shard_map/ppermute | solution.py:303
  12.3 0.0 collective-permute-done.1.rows_b_ref
  12.3 0.0 copy-start.2
  12.3 0.0 collective-permute-done.rows_a_ref
  12.4 0.0 copy-start.3
  12.4 0.0 collective-permute-done.3.cols_b_ref
  12.4 0.0 copy-start.4
  12.4 1.0 %collective-permute-done.2.cols_a_ref = f32[24,128]{1,0:T(8,128)S(1)} collective-permute-done((f32[24,128]{1,0:T(8,128)}, f32[24,128]{1,0:T(8,128)S(1)}, u32[]{:S(2)}, u32[]{:S(2)}) %collective-permute-start.2) | collective-permute-done | bytes 12320 | tf_op jit(solution)/shard_map/ppermute | solution.py:303
  13.4 0.0 copy-done.2
  13.4 0.0 copy-done.3
  13.4 0.0 copy-done.4
  13.4 0.0 copy-start.5
  13.4 0.6 %copy-done.5 = f32[24,128]{1,0:T(8,128)} copy-done((f32[24,128]{1,0:T(8,128)}, f32[24,128]{1,0:T(8,128)S(1)}, u32[]{:S(2)}) %copy-start.5) | copy-done | bytes 12312
  14.0 2.4 %shard_map.114 = f32[72,256]{1,0:T(8,128)} custom-call(s32[1,64]{1,0:T(1,128)} %flags_ref.1, s32[1,64]{1,0:T(1,128)} %flags_ref.1, f32[128,128]{1,0:T(8,128)} %open_ref.3, f32[128,128]{1,0:T(8,128)} %press_ref.3, f32[128,128]{1,0:T(8,128)} %inject_ref.3, f32[24,128]{1,0:T(8,128)} %copy-done.3, f32[24,128]{1,0:T(8,128)} %copy-done.2, f32[24,128]{1,0:T(8,128)} %copy-done.5, ...), custom_call_target="tpu_custom_call" | custom-call | tf_op jit(solution)/shard_map/pallas_call | solution.py:304
  16.4 4.7 %collective-permute-start.6 = (f32[72,256]{1,0:T(8,128)}, f32[72,256]{1,0:T(8,128)S(1)}, u32[]{:S(2)}, u32[]{:S(2)}) collective-permute-start(f32[72,256]{1,0:T(8,128)} %shard_map.114), channel_id=1, source_target_pairs={{0,6},{1,7},{2,4},{3,5},{4,2},{5,3},{6,0},{7,1},{8,14},{9,15},{10,... | collective-permute-start | bytes 221192 | tf_op jit(solution)/shard_map/ppermute | solution.py:322
  21.1 0.0 collective-permute-start.5
  21.1 0.6 %collective-permute-start.4 = (f32[72,256]{1,0:T(8,128)}, f32[72,256]{1,0:T(8,128)S(1)}, u32[]{:S(2)}, u32[]{:S(2)}) collective-permute-start(f32[72,256]{1,0:T(8,128)} %shard_map.114), channel_id=1, source_target_pairs={{0,2},{1,3},{2,0},{3,1},{4,6},{5,7},{6,4},{7,5},{8,10},{9,11},{10,... | collective-permute-start | bytes 221192 | tf_op jit(solution)/shard_map/ppermute | solution.py:322
  21.7 2.2 %collective-permute-done.6 = f32[72,256]{1,0:T(8,128)S(1)} collective-permute-done((f32[72,256]{1,0:T(8,128)}, f32[72,256]{1,0:T(8,128)S(1)}, u32[]{:S(2)}, u32[]{:S(2)}) %collective-permute-start.6) | collective-permute-done | bytes 73760 | tf_op jit(solution)/shard_map/ppermute | solution.py:322
  23.8 3.9 %collective-permute-done.5 = f32[72,256]{1,0:T(8,128)S(1)} collective-permute-done((f32[72,256]{1,0:T(8,128)}, f32[72,256]{1,0:T(8,128)S(1)}, u32[]{:S(2)}, u32[]{:S(2)}) %collective-permute-start.5) | collective-permute-done | bytes 73760 | tf_op jit(solution)/shard_map/ppermute | solution.py:322
  27.7 0.0 collective-permute-done.4
  27.7 0.9 %pad_maximum_fusion.near_ref = f32[288,256]{1,0:T(8,128)S(1)} fusion(f32[72,256]{1,0:T(8,128)S(1)} %collective-permute-done.6, f32[72,256]{1,0:T(8,128)S(1)} %collective-permute-done.5, f32[72,256]{1,0:T(8,128)S(1)} %collective-permute-done.4, f32[72,256]{1,0:T(8,128)} %shard_map.114), kind=kLoop, calls=%fused_computation | loop fusion | flops 221184 | bytes 589824 | tf_op jit(solution)/shard_map/concatenate | solution.py:324
  28.7 0.0 copy-start
  28.7 0.1 collective-permute-start.7
  28.7 1.6 %collective-permute-done.7.far_ref = f32[288,256]{1,0:T(8,128)S(1)} collective-permute-done((f32[288,256]{1,0:T(8,128)S(1)}, f32[288,256]{1,0:T(8,128)S(1)}, u32[]{:S(2)}, u32[]{:S(2)}) %collective-permute-start.7) | collective-permute-done | bytes 294944 | tf_op jit(solution)/shard_map/ppermute | solution.py:322
  30.3 0.0 copy-start.1
  30.3 0.0 copy-done
  30.3 0.7 %copy-done.1 = f32[288,256]{1,0:T(8,128)} copy-done((f32[288,256]{1,0:T(8,128)}, f32[288,256]{1,0:T(8,128)S(1)}, u32[]{:S(2)}) %copy-start.1) | copy-done | bytes 294936
  31.0 7.9 %shard_map.115 = (f32[128,128]{1,0:T(8,128)}, f32[128,128]{1,0:T(8,128)}) custom-call(s32[4,64]{1,0:T(4,128)} %bitcast.13, s32[4,64]{1,0:T(4,128)} %bitcast.14, s32[4,64]{1,0:T(4,128)} %bitcast.15, f32[288,256]{1,0:T(8,128)} %copy-done, f32[288,256]{1,0:T(8,128)} %copy-done.1, f32[256,256]{1,0:T(8,128)} %self_ref.1, f32[64,4,16,256]{3,2,1,0:T(8,128)} %bitcast.11, ...), custom_call_target="tpu_custom_call" | custom-call | tf_op jit(solution)/shard_map/pallas_call | solution.py:326
Async XLA Ops:
  2.3 10.1 %collective-permute-start.1 = (f32[24,128]{1,0:T(8,128)}, f32[24,128]{1,0:T(8,128)S(1)}, u32[]{:S(2)}, u32[]{:S(2)}) collective-permute-start(f32[24,128]{1,0:T(8,128)} %get-tuple-element.4), channel_id=1, source_target_pairs={{0,0},{8,16},{16,8},{24,24},{1,1},{9,17},{17,9},{25,25},{2,2},{10,... | collective-permute-start | bytes 36872 | tf_op jit(solution)/shard_map/ppermute | solution.py:300
  3.6 8.7 %collective-permute-start = (f32[24,128]{1,0:T(8,128)}, f32[24,128]{1,0:T(8,128)S(1)}, u32[]{:S(2)}, u32[]{:S(2)}) collective-permute-start(f32[24,128]{1,0:T(8,128)} %get-tuple-element.4), channel_id=1, source_target_pairs={{0,8},{8,0},{16,24},{24,16},{1,9},{9,1},{17,25},{25,17},{2,10},{10... | collective-permute-start | bytes 36872 | tf_op jit(solution)/shard_map/ppermute | solution.py:301
  8.7 3.7 %collective-permute-start.3 = (f32[24,128]{1,0:T(8,128)}, f32[24,128]{1,0:T(8,128)S(1)}, u32[]{:S(2)}, u32[]{:S(2)}) collective-permute-start(f32[24,128]{1,0:T(8,128)} %get-tuple-element.5), channel_id=1, source_target_pairs={{0,0},{1,2},{2,1},{3,4},{4,3},{5,6},{6,5},{7,7},{8,8},{9,10},{10,9... | collective-permute-start | bytes 36872 | tf_op jit(solution)/shard_map/ppermute | solution.py:302
  10.0 3.4 %collective-permute-start.2 = (f32[24,128]{1,0:T(8,128)}, f32[24,128]{1,0:T(8,128)S(1)}, u32[]{:S(2)}, u32[]{:S(2)}) collective-permute-start(f32[24,128]{1,0:T(8,128)} %get-tuple-element.5), channel_id=1, source_target_pairs={{0,1},{1,0},{2,3},{3,2},{4,5},{5,4},{6,7},{7,6},{8,9},{9,8},{10,11... | collective-permute-start | bytes 36872 | tf_op jit(solution)/shard_map/ppermute | solution.py:303
  12.3 1.0 %copy-start.2 = (f32[24,128]{1,0:T(8,128)}, f32[24,128]{1,0:T(8,128)S(1)}, u32[]{:S(2)}) copy-start(f32[24,128]{1,0:T(8,128)S(1)} %collective-permute-done.1.rows_b_ref) | copy-start | bytes 36868
  12.4 1.0 %copy-start.3 = (f32[24,128]{1,0:T(8,128)}, f32[24,128]{1,0:T(8,128)S(1)}, u32[]{:S(2)}) copy-start(f32[24,128]{1,0:T(8,128)S(1)} %collective-permute-done.rows_a_ref) | copy-start | bytes 36868
  12.4 1.0 %copy-start.4 = (f32[24,128]{1,0:T(8,128)}, f32[24,128]{1,0:T(8,128)S(1)}, u32[]{:S(2)}) copy-start(f32[24,128]{1,0:T(8,128)S(1)} %collective-permute-done.3.cols_b_ref) | copy-start | bytes 36868
  13.4 0.6 %copy-start.5 = (f32[24,128]{1,0:T(8,128)}, f32[24,128]{1,0:T(8,128)S(1)}, u32[]{:S(2)}) copy-start(f32[24,128]{1,0:T(8,128)S(1)} %collective-permute-done.2.cols_a_ref) | copy-start | bytes 36868
  16.4 7.4 %collective-permute-start.6 = (f32[72,256]{1,0:T(8,128)}, f32[72,256]{1,0:T(8,128)S(1)}, u32[]{:S(2)}, u32[]{:S(2)}) collective-permute-start(f32[72,256]{1,0:T(8,128)} %shard_map.114), channel_id=1, source_target_pairs={{0,6},{1,7},{2,4},{3,5},{4,2},{5,3},{6,0},{7,1},{8,14},{9,15},{10,... | collective-permute-start | bytes 221192 | tf_op jit(solution)/shard_map/ppermute | solution.py:322
  21.1 6.7 %collective-permute-start.5 = (f32[72,256]{1,0:T(8,128)}, f32[72,256]{1,0:T(8,128)S(1)}, u32[]{:S(2)}, u32[]{:S(2)}) collective-permute-start(f32[72,256]{1,0:T(8,128)} %shard_map.114), channel_id=1, source_target_pairs={{0,4},{1,5},{2,6},{3,7},{4,0},{5,1},{6,2},{7,3},{8,12},{9,13},{10,... | collective-permute-start | bytes 221192 | tf_op jit(solution)/shard_map/ppermute | solution.py:322
  21.1 6.7 %collective-permute-start.4 = (f32[72,256]{1,0:T(8,128)}, f32[72,256]{1,0:T(8,128)S(1)}, u32[]{:S(2)}, u32[]{:S(2)}) collective-permute-start(f32[72,256]{1,0:T(8,128)} %shard_map.114), channel_id=1, source_target_pairs={{0,2},{1,3},{2,0},{3,1},{4,6},{5,7},{6,4},{7,5},{8,10},{9,11},{10,... | collective-permute-start | bytes 221192 | tf_op jit(solution)/shard_map/ppermute | solution.py:322
  28.7 1.7 %copy-start = (f32[288,256]{1,0:T(8,128)}, f32[288,256]{1,0:T(8,128)S(1)}, u32[]{:S(2)}) copy-start(f32[288,256]{1,0:T(8,128)S(1)} %pad_maximum_fusion.near_ref) | copy-start | bytes 884740
  28.7 1.6 %collective-permute-start.7 = (f32[288,256]{1,0:T(8,128)S(1)}, f32[288,256]{1,0:T(8,128)S(1)}, u32[]{:S(2)}, u32[]{:S(2)}) collective-permute-start(f32[288,256]{1,0:T(8,128)S(1)} %pad_maximum_fusion.near_ref), channel_id=1, source_target_pairs={{0,1},{1,0},{2,3},{3,2},{4,5},{5,4},{6,7},{7,6},{8,9},{9,8},{10,11... | collective-permute-start | bytes 884744 | tf_op jit(solution)/shard_map/ppermute | solution.py:322
  30.3 0.7 %copy-start.1 = (f32[288,256]{1,0:T(8,128)}, f32[288,256]{1,0:T(8,128)S(1)}, u32[]{:S(2)}) copy-start(f32[288,256]{1,0:T(8,128)S(1)} %collective-permute-done.7.far_ref) | copy-start | bytes 884740

commit v2 on v1

v2 whole, which is shorter than its diff:
```python
import functools

import jax
import jax.numpy as jnp
from jax import lax
from jax.experimental import pallas as pl
from jax.experimental.pallas import tpu as pltpu
from jax.sharding import PartitionSpec as P


TSIDE = 16
PASSES = 3
GROUP = 8
LANES = 128
SUB = 8
step_size = 0.1


def neighbour_pairs(count, first):
    pairs = [(i, i) for i in range(count)]
    for i in range(first, count - 1, 2):
        pairs[i], pairs[i + 1] = (i, i + 1), (i + 1, i)
    return pairs


def iota(shape, axis):
    return lax.broadcasted_iota(jnp.int32, shape, axis)


def edges_kernel(open_ref, press_ref, inject_ref, fields_ref, rows_ref, cols_ref, sems):
    sub = iota((SUB, LANES), 0)
    lane = iota((SUB, LANES), 1)
    rows = open_ref.shape[0]
    copies = [
        pltpu.make_async_copy(ref, fields_ref.at[f], sems.at[f])
        for f, ref in enumerate((open_ref, press_ref, inject_ref))
    ]
    for copy in copies:
        copy.start()
    for f, copy in enumerate(copies):
        copy.wait()
        ref = fields_ref.at[f]
        rows_ref[f * SUB : (f + 1) * SUB, :] = jnp.where(
            sub < SUB // 2, ref[0:SUB, :], ref[rows - SUB : rows, :]
        )
        packed = jnp.zeros((SUB, LANES), jnp.float32)
        for g in range(rows // SUB):
            moved = pltpu.roll(ref[g * SUB : (g + 1) * SUB, :], (3 + 8 * g) % LANES, 1)
            packed = jnp.where(lane // 8 == g, moved, packed)
        cols_ref[f * SUB : (f + 1) * SUB, :] = packed


def swap_groups(value):
    sub = iota(value.shape, value.ndim - 2)
    group = iota(value.shape, value.ndim - 1) // TSIDE
    row_axis, lane_axis = value.ndim - 2, value.ndim - 1
    for d in (1, 2, 4):
        low_row, low_group = (sub & d) == 0, (group & d) == 0
        up = pltpu.roll(pltpu.roll(value, SUB - d, row_axis), TSIDE * d, lane_axis)
        down = pltpu.roll(pltpu.roll(value, d, row_axis), LANES - TSIDE * d, lane_axis)
        value = jnp.where(
            low_row == low_group, value, jnp.where(low_row, up, down)
        )
    return value


def picard(opening, pressure, inject, inside):
    rows, cols = opening.shape[-2:]
    row_axis, col_axis = opening.ndim - 2, opening.ndim - 1
    shifts = ((row_axis, rows - 1), (row_axis, 1), (col_axis, cols - 1), (col_axis, 1))
    pressure = jnp.where(inside, pressure, 0.0)
    opening = jnp.where(inside, opening, 0.0)
    base = jnp.where(inside, opening + step_size * inject, 0.0)
    slopes = [
        jnp.where(inside, (pltpu.roll(pressure, s, a) - pressure) * (step_size / 24.0), 0.0)
        for a, s in shifts
    ]
    current = opening
    for _ in range(PASSES):
        cubed = current * current * current
        current = base
        for (a, s), slope in zip(shifts, slopes):
            current = current + (cubed + pltpu.roll(cubed, s, a)) * slope
    return current


def stencil_kernel(
    counts,
    flag_ref,
    flags_ref,
    fields_ref,
    rows_a_ref,
    rows_b_ref,
    cols_a_ref,
    cols_b_ref,
    column_ref,
    tile_ref,
    out_ref,
    index_ref,
):
    n_row, n_col = counts
    rows, cols = fields_ref.shape[1:]
    old = [fields_ref.at[f] for f in range(3)]
    wide, tall = cols + LANES, rows + SUB
    me_row, me_col = lax.axis_index("row"), lax.axis_index("col")
    row_even, col_even = me_row % 2 == 0, me_col % 2 == 0
    sub = iota((SUB, LANES), 0)
    lane = iota((SUB, LANES), 1)
    fields, tails = [], []
    for f, ref in enumerate(old):
        part = slice(f * SUB, (f + 1) * SUB)
        below = jnp.where(row_even, rows_a_ref[part, :], rows_b_ref[part, :])
        above = jnp.where(row_even, rows_b_ref[part, :], rows_a_ref[part, :])
        tail = jnp.where(sub < SUB // 2, below, above)
        right = jnp.where(col_even, cols_a_ref[part, :], cols_b_ref[part, :])
        left = jnp.where(col_even, cols_b_ref[part, :], cols_a_ref[part, :])
        packed = jnp.where(lane % 8 < 3, left, right)
        sides = []
        for g in range(rows // SUB):
            moved = pltpu.roll(packed, (LANES - 3 - 8 * g) % LANES, 1)
            sides.append(jnp.where((lane < 3) | (lane >= LANES - 3), moved, 0.0))
        sides.append(jnp.zeros((SUB, LANES), jnp.float32))
        main = jnp.concatenate([ref[...], tail], axis=0)
        fields.append(jnp.concatenate([main, jnp.concatenate(sides, axis=0)], axis=1))
        tails.append(tail)
    row = iota((tall, wide), 0)
    col = iota((tall, wide), 1)
    row = me_row * rows + jnp.where(row < rows + SUB // 2, row, row - tall)
    col = me_col * cols + jnp.where(col < cols + LANES // 2, col, col - wide)
    inside = (row >= 0) & (row < n_row * rows) & (col >= 0) & (col < n_col * cols)
    current = picard(*fields, inside)[:rows, :cols]
    tiles = swap_groups(current.reshape(rows // SUB, SUB, LANES))
    count = flags_ref.shape[1]
    ones = jnp.where(iota((count, count), 0) == iota((count, count), 1), flags_ref[...], 0)
    flags = jnp.sum(ones.astype(jnp.float32), axis=1, keepdims=True)
    for a in range(rows // TSIDE):
        for h in range(2):
            at = h * count + a * SUB
            out_ref[at : at + SUB, :] = tiles[2 * a + h] * flags[a * SUB : a * SUB + SUB, :]
    corner = jnp.zeros((SUB, LANES), jnp.float32)
    for f, ref in enumerate(old):
        top = pltpu.roll(jnp.where(sub < 5, ref[0:SUB, :], tails[f]), 3, 0)
        bottom = pltpu.roll(jnp.where(sub >= 3, ref[rows - SUB : rows, :], tails[f]), 5, 0)
        for b, window in enumerate((top, bottom)):
            at = (f * 2 + b) * 10
            corner = jnp.where(
                (lane >= at + 5) & (lane < at + 10), pltpu.roll(window, at + 5, 1), corner
            )
            corner = jnp.where(
                (lane >= 64 + at) & (lane < 69 + at),
                pltpu.roll(window, (64 + at - (LANES - 5)) % LANES, 1),
                corner,
            )
    side = cols // TSIDE
    for at, tile in ((0, 0), (10, count - side), (69, side - 1), (79, count - 1)):
        corner = jnp.where(
            (lane >= at) & (lane < at + 5), flag_ref[0, tile].astype(jnp.float32), corner
        )
    out_ref[2 * count :, :] = corner
    step = column_ref[...] ^ me_col
    index_ref[...] = ((step >> 1) + (step & 1) * (n_col // 2)) * count + tile_ref[...]


def split_dot(left, right):
    dims = (((1,), (1,)), ((), ()))

    def dot(a, b):
        return lax.dot_general(a, b, dims, preferred_element_type=jnp.float32)

    left_high = left.astype(jnp.bfloat16)
    left_low = (left - left_high.astype(jnp.float32)).astype(jnp.bfloat16)
    right_high = right.astype(jnp.bfloat16)
    right_low = (right - right_high.astype(jnp.float32)).astype(jnp.bfloat16)
    return dot(left_high, right_high) + (dot(left_high, right_low) + dot(left_low, right_high))


def pressure_kernel(counts, index_ref, rank_ref, *refs):
    n_row, n_col = counts
    blocks = refs[:n_col]
    self_ref, right_ref, left_ref, open_out, press_out, band, base, press, around, fixes = refs[n_col:]
    me_row, me_col = lax.axis_index("row"), lax.axis_index("col")
    count = press.shape[1]
    rows, cols = open_out.shape
    sub = iota((SUB, LANES), 0)
    lane = iota((SUB, LANES), 1)
    steps = [2 * i for i in range(n_col // 2)] + [2 * i + 1 for i in range(n_col // 2)]
    columns = [me_col ^ step for step in steps]

    for ref, column in zip(blocks, columns):
        around[pl.ds(pl.multiple_of(column * SUB, SUB), SUB), :] = ref[2 * count :, :]
    corners = [around[c * SUB : (c + 1) * SUB, :] for c in range(n_col)]
    outside = ((sub < 3) & (lane < 10) & (me_row == 0)) | (
        (sub >= 5) & (lane >= 10) & (me_row == n_row - 1)
    )
    left_part = (lane % 10) < 5
    for c in range(n_col - 1):
        a, b = corners[c], corners[c + 1]
        window = jnp.where(left_part, pltpu.roll(a, 64, 1), b)
        marks = jnp.where(left_part, pltpu.roll(a, 59, 1), pltpu.roll(b, 5, 1))
        fixed = picard(
            window,
            pltpu.roll(window, LANES - 20, 1),
            pltpu.roll(window, LANES - 40, 1),
            jnp.logical_not(outside),
        )
        fixes[c * SUB : (c + 1) * SUB, :] = fixed * marks

    def patch(value, fixed, when, moves):
        for row, at, to_row, to, wide in moves:
            moved = pltpu.roll(pltpu.roll(fixed, (to_row - row) % SUB, 0), (to - at) % LANES, 1)
            value = jnp.where(
                (sub == to_row) & (lane >= to) & (lane < to + wide) & when, moved, value
            )
        return value

    last = SUB - 1
    for slot, (ref, column) in enumerate(zip(blocks, columns)):
        before = fixes[pl.ds(pl.multiple_of(jnp.maximum(column - 1, 0) * SUB, SUB), SUB), :]
        after = fixes[pl.ds(pl.multiple_of(jnp.minimum(column, n_col - 2) * SUB, SUB), SUB), :]
        first, final = column > 0, column < n_col - 1
        top = patch(ref[0:SUB, :], before, first, ((3, 5, 0, 0, 2), (4, 5, 0, 16, 1)))
        top = patch(top, after, final, ((3, 3, last, 14, 2), (4, 4, last, 31, 1)))
        bottom = ref[2 * count - SUB : 2 * count, :]
        bottom = patch(bottom, before, first, ((4, 15, 0, 112, 2), (3, 15, 0, 96, 1)))
        bottom = patch(bottom, after, final, ((4, 13, last, 126, 2), (3, 14, last, 111, 1)))
        lower = jnp.concatenate([top, ref[SUB:count, :]], axis=0)
        upper = jnp.concatenate([ref[count : 2 * count - SUB, :], bottom], axis=0)
        band[0, slot * count : (slot + 1) * count, :] = lower
        band[1, slot * count : (slot + 1) * count, :] = upper
        if slot == 0:
            own = (lower, upper)

    def lay_out(lower, upper):
        parts = [
            half[SUB * a : SUB * a + SUB, :] for a in range(rows // TSIDE) for half in (lower, upper)
        ]
        return swap_groups(jnp.stack(parts)).reshape(rows, cols)

    open_out[...] = lay_out(*own)
    base[...] = split_dot(jnp.concatenate(own, axis=1), self_ref[...])

    links, ranks = right_ref.shape[1], right_ref.shape[2]
    depth = iota((ranks, LANES), 0)

    def targets(group, carry):
        for i in range(GROUP):
            t = group * GROUP + i
            total = [jnp.zeros((ranks, LANES), jnp.float32)] * 2
            for k in range(links):
                at = index_ref[k, t]
                product = sum(
                    right_ref[t, k, :, h * LANES : (h + 1) * LANES] * band[h, pl.ds(at, 1), :]
                    for h in range(2)
                )
                coefficient = jnp.sum(product, axis=1, keepdims=True)
                coefficient = jnp.where(depth < rank_ref[k, t], coefficient, 0.0)
                total = [
                    total[h] + left_ref[t, k, :, h * LANES : (h + 1) * LANES] * coefficient
                    for h in range(2)
                ]
            for h in range(2):
                press[h, pl.ds(t, 1), :] = jnp.sum(total[h], axis=0, keepdims=True)
        return carry

    lax.fori_loop(0, count // GROUP, targets, 0)
    press_out[...] = lay_out(*(press[h] + base[:, h * LANES : (h + 1) * LANES] for h in range(2)))


def local(
    opening_old,
    pressure_old,
    injection,
    front_flags,
    self_kernel,
    source_column,
    source_tile,
    source_rank,
    left_factor,
    right_factor,
):
    n_row, n_col = lax.axis_size("row"), lax.axis_size("col")
    counts = (n_row, n_col)
    rows, cols = opening_old.shape
    count = front_flags.shape[1]
    links = source_column.shape[2]
    vmem = pl.BlockSpec(memory_space=pltpu.VMEM)
    smem = pl.BlockSpec(memory_space=pltpu.SMEM)
    f32 = jnp.float32

    def held(value):
        return pltpu.with_memory_space_constraint(value, pltpu.VMEM)

    fields, edge_rows, edge_cols = pl.pallas_call(
        edges_kernel,
        out_shape=[pltpu.VMEM((3, rows, cols), f32)] + [pltpu.VMEM((3 * SUB, LANES), f32)] * 2,
        in_specs=[pl.BlockSpec(memory_space=pltpu.HBM)] * 3,
        out_specs=[vmem] * 3,
        scratch_shapes=[pltpu.SemaphoreType.DMA((3,))],
        compiler_params=pltpu.CompilerParams(vmem_limit_bytes=4 << 20),
        cost_estimate=pl.CostEstimate(flops=4_000_000_000, transcendentals=0, bytes_accessed=30_000_000),
    )(*(pltpu.with_memory_space_constraint(x, pltpu.HBM) for x in (opening_old, pressure_old, injection)))
    rows_b = lax.ppermute(edge_rows, "row", neighbour_pairs(n_row, 1))
    rows_a = lax.ppermute(edge_rows, "row", neighbour_pairs(n_row, 0))
    cols_b = lax.ppermute(edge_cols, "col", neighbour_pairs(n_col, 1))
    cols_a = lax.ppermute(edge_cols, "col", neighbour_pairs(n_col, 0))
    block, index = pl.pallas_call(
        functools.partial(stencil_kernel, counts),
        out_shape=[
            pltpu.VMEM((2 * count + SUB, LANES), f32),
            pltpu.VMEM((links, count), jnp.int32),
        ],
        in_specs=[smem] + [vmem] * 8,
        out_specs=[vmem] * 2,
        compiler_params=pltpu.CompilerParams(vmem_limit_bytes=4 << 20),
        cost_estimate=pl.CostEstimate(
            flops=4_000_000_000, transcendentals=0, bytes_accessed=30_000_000
        ),
    )(
        front_flags,
        front_flags,
        held(fields),
        held(rows_a),
        held(rows_b),
        held(cols_a),
        held(cols_b),
        source_column[0].T,
        source_tile[0].T,
    )

    def exchange(value, step):
        return lax.ppermute(value, "col", [(i, i ^ step) for i in range(n_col)])

    near = [block] + [exchange(block, step) for step in range(2, n_col, 2)]
    far = [exchange(value, 1) for value in near]
    opening_new, pressure_new = pl.pallas_call(
        functools.partial(pressure_kernel, counts),
        out_shape=[jax.ShapeDtypeStruct((rows, cols), f32)] * 2,
        in_specs=[smem] * 2 + [vmem] * (n_col + 3),
        out_specs=[vmem] * 2,
        scratch_shapes=[
            pltpu.VMEM((2, n_col * count, LANES), f32),
            pltpu.VMEM((count, 2 * LANES), f32),
            pltpu.VMEM((2, count, LANES), f32),
            pltpu.VMEM((n_col * SUB, LANES), f32),
            pltpu.VMEM((n_col * SUB, LANES), f32),
        ],
        compiler_params=pltpu.CompilerParams(vmem_limit_bytes=8 << 20),
    )(
        index,
        source_rank[0].T,
        *(held(value) for value in near + far),
        self_kernel,
        right_factor[0],
        left_factor[0],
    )
    return opening_new, pressure_new


def solution(mesh):
    return jax.shard_map(
        local,
        mesh=mesh,
        in_specs=(
            P("row", "col"),
            P("row", "col"),
            P("row", "col"),
            P("row", "col"),
            P(),
            P("row", "col", None),
            P("row", "col", None),
            P("row", "col", None),
            P("row", "col", None, None, None),
            P("row", "col", None, None, None),
        ),
        out_specs=(P("row", "col"), P("row", "col")),
        check_vma=False,
    )
```

time: 39.3 us -> 29.6 us (0.75)
  Pallas kernels: 11.9 us -> 6.08 us
  waiting for transfers between devices: 8.66 us -> 7.18 us
  local copies, waits for them, and re-layouts: 1.32 us -> 0.04 us
  other arithmetic: 0.91 us -> 0 us
    pallas_call x1, Pallas kernels: 7.87 us -> 3.57 us  [local(): pl.pallas_call(functools.partial(pressure_kernel, counts), out_shape=[jax...]
    pallas_call x2, Pallas kernels: 4.02 us -> 2.51 us  [the longest x1 1.37 us: local(): pl.pallas_call(functools.partial(stencil_kernel, counts), out_shape=[pltp...]
    ppermute x4 -> x7, waiting for transfers between devices: 7.65 us -> 6.35 us  [exchange(): return lax.ppermute(value, 'col', [(i, i ^ step) for i in range(n_col)])]
    unnamed x12 -> x14, local copies, waits for them, and re-layouts: 1.32 us -> 0.04 us
    concatenate x1 -> x0, other arithmetic: 0.91 us -> none  [local(): jnp.concatenate([block] + [exchange(block, s) for s in range(2, n_col, 2)...]
    ppermute x1, starting transfers between devices: 1.35 us -> 0.65 us  [local(): cols_b = lax.ppermute(edge_cols, 'col', neighbour_pairs(n_col, 1))]
    ppermute x1, starting transfers between devices: 2.31 us -> 3 us  [local(): cols_a = lax.ppermute(edge_cols, 'col', neighbour_pairs(n_col, 0))]
    ppermute x1, starting transfers between devices: 5.07 us -> 5.77 us  [local(): rows_a = lax.ppermute(edge_rows, 'row', neighbour_pairs(n_row, 0))]
  transfers between devices with their start and end apart: 8 -> 11, of which waited for: 4 -> 5; matrix products, arithmetic and copies ran while one was open for 0% -> 0% of each run, Pallas kernels for 0% -> 0%
where the time goes in v2:
time: 29.6 us; the launch traced here: 29.5 us
  starting transfers between devices  15.4 us (52%)
  waiting for transfers between devices  7.18 us (24%)
  Pallas kernels  6.08 us (21%)
  between operations  0.73 us (2%)
    ppermute x7, waiting for transfers between devices, exchange(): return lax.ppermute(value, 'col', [(i, i ^ step) for i in range(n_col)])  6.35 us
    ppermute x1, starting transfers between devices, local(): rows_a = lax.ppermute(edge_rows, 'row', neighbour_pairs(n_row, 0))  5.77 us
    ppermute x7, starting transfers between devices, exchange(): return lax.ppermute(value, 'col', [(i, i ^ step) for i in range(n_col)])  5.35 us
    pallas_call x1, Pallas kernels, local(): pl.pallas_call(functools.partial(pressure_kernel, counts), out_shape=[jax...  3.57 us
    ppermute x1, starting transfers between devices, local(): cols_a = lax.ppermute(edge_cols, 'col', neighbour_pairs(n_col, 0))  3 us
    pallas_call x1, Pallas kernels, local(): pl.pallas_call(functools.partial(stencil_kernel, counts), out_shape=[pltp...  1.37 us
    pallas_call x1, Pallas kernels, local(): pl.pallas_call(edges_kernel, out_shape=[pltpu.VMEM((3, rows, cols), f32)]...  1.14 us
    ppermute x1, waiting for transfers between devices, local(): cols_a = lax.ppermute(edge_cols, 'col', neighbour_pairs(n_col, 0))  0.82 us
  transfers between devices with their start and end apart: 11, of which 5 were waited for; matrix products, arithmetic and copies ran while one was open for 0% of the time, Pallas kernels for 0%

profile of v2, /device:TPU:0, one launch (start us, length us, event | category | flops | bytes accessed | tf_op | source)
XLA Modules:
  0.0 29.5 jit_solution(4171236370023999918)
XLA Ops:
  0.6 0.0 copy-start.5
  0.6 0.0 copy-start.4
  0.7 1.1 %shard_map.113 = (f32[3,128,128]{2,1,0:T(8,128)S(1)}, f32[24,128]{1,0:T(8,128)S(1)}, f32[24,128]{1,0:T(8,128)S(1)}) custom-call(f32[128,128]{1,0:T(8,128)} %open_ref.1, f32[128,128]{1,0:T(8,128)} %press_ref.1, f32[128,128]{1,0:T(8,128)} %inject_ref.1), custom_call_target="tpu_custom_call" | custom-call | flops 4000000000 | bytes 30000000 | tf_op jit(solution)/shard_map/pallas_call | solution.py:293
  1.8 0.7 %collective-permute-start.1 = (f32[24,128]{1,0:T(8,128)S(1)}, f32[24,128]{1,0:T(8,128)S(1)}, u32[]{:S(2)}, u32[]{:S(2)}) collective-permute-start(f32[24,128]{1,0:T(8,128)S(1)} %get-tuple-element.8), channel_id=1, source_target_pairs={{0,0},{8,16},{16,8},{24,24},{1,1},{9,17},{17,9},{25,25},{2,2},{10,... | collective-permute-start | bytes 36872 | tf_op jit(solution)/shard_map/ppermute | solution.py:302
  2.5 5.8 %collective-permute-start = (f32[24,128]{1,0:T(8,128)S(1)}, f32[24,128]{1,0:T(8,128)S(1)}, u32[]{:S(2)}, u32[]{:S(2)}) collective-permute-start(f32[24,128]{1,0:T(8,128)S(1)} %get-tuple-element.8), channel_id=1, source_target_pairs={{0,8},{8,0},{16,24},{24,16},{1,9},{9,1},{17,25},{25,17},{2,10},{10... | collective-permute-start | bytes 36872 | tf_op jit(solution)/shard_map/ppermute | solution.py:303
  8.2 0.7 %collective-permute-start.3 = (f32[24,128]{1,0:T(8,128)S(1)}, f32[24,128]{1,0:T(8,128)S(1)}, u32[]{:S(2)}, u32[]{:S(2)}) collective-permute-start(f32[24,128]{1,0:T(8,128)S(1)} %get-tuple-element.9), channel_id=1, source_target_pairs={{0,0},{1,2},{2,1},{3,4},{4,3},{5,6},{6,5},{7,7},{8,8},{9,10},{10,9... | collective-permute-start | bytes 36872 | tf_op jit(solution)/shard_map/ppermute | solution.py:304
  8.9 3.0 %collective-permute-start.2 = (f32[24,128]{1,0:T(8,128)S(1)}, f32[24,128]{1,0:T(8,128)S(1)}, u32[]{:S(2)}, u32[]{:S(2)}) collective-permute-start(f32[24,128]{1,0:T(8,128)S(1)} %get-tuple-element.9), channel_id=1, source_target_pairs={{0,1},{1,0},{2,3},{3,2},{4,5},{5,4},{6,7},{7,6},{8,9},{9,8},{10,11... | collective-permute-start | bytes 36872 | tf_op jit(solution)/shard_map/ppermute | solution.py:305
  11.9 0.0 collective-permute-done.1.rows_b_ref
  11.9 0.0 collective-permute-done.rows_a_ref
  11.9 0.0 collective-permute-done.3.cols_b_ref
  11.9 0.8 %collective-permute-done.2.cols_a_ref = f32[24,128]{1,0:T(8,128)S(1)} collective-permute-done((f32[24,128]{1,0:T(8,128)S(1)}, f32[24,128]{1,0:T(8,128)S(1)}, u32[]{:S(2)}, u32[]{:S(2)}) %collective-permute-start.2) | collective-permute-done | bytes 12320 | tf_op jit(solution)/shard_map/ppermute | solution.py:305
  12.7 0.0 copy-done.4
  12.8 0.0 copy-start.1
  12.8 0.0 copy-start.2
  12.8 0.0 copy-start.3
  12.8 1.4 %shard_map.114 = (f32[136,128]{1,0:T(8,128)S(1)}, s32[4,64]{1,0:T(4,128)S(1)}) custom-call(s32[1,64]{1,0:T(1,128)S(1)} %copy-done.6, s32[1,64]{1,0:T(1,128)S(1)} %copy-done.6, f32[3,128,128]{2,1,0:T(8,128)S(1)} %get-tuple-element.7.fields_ref, f32[24,128]{1,0:T(8,128)S(1)} %collective-permute-done.rows_a_ref, ...), custom_call_target="tpu_custom_call" | custom-call | flops 4000000000 | bytes 30000000 | tf_op jit(solution)/shard_map/pallas_call | solution.py:306
  14.2 4.2 %collective-permute-start.6 = (f32[136,128]{1,0:T(8,128)S(1)}, f32[136,128]{1,0:T(8,128)S(1)}, u32[]{:S(2)}, u32[]{:S(2)}) collective-permute-start(f32[136,128]{1,0:T(8,128)S(1)} %get-tuple-element.11.refs_0_), channel_id=1, source_target_pairs={{0,6},{1,7},{2,4},{3,5},{4,2},{5,3},{6,0},{7,1},{8,14},{9,15},{10,... | collective-permute-start | bytes 208904 | tf_op jit(solution)/shard_map/ppermute | solution.py:331
  18.4 0.0 collective-permute-start.5
  18.4 0.6 %collective-permute-start.4 = (f32[136,128]{1,0:T(8,128)S(1)}, f32[136,128]{1,0:T(8,128)S(1)}, u32[]{:S(2)}, u32[]{:S(2)}) collective-permute-start(f32[136,128]{1,0:T(8,128)S(1)} %get-tuple-element.11.refs_0_), channel_id=1, source_target_pairs={{0,2},{1,3},{2,0},{3,1},{4,6},{5,7},{6,4},{7,5},{8,10},{9,11},{10,... | collective-permute-start | bytes 208904 | tf_op jit(solution)/shard_map/ppermute | solution.py:331
  19.0 0.0 collective-permute-start.7
  19.0 1.8 %collective-permute-done.6.refs_3_ = f32[136,128]{1,0:T(8,128)S(1)} collective-permute-done((f32[136,128]{1,0:T(8,128)S(1)}, f32[136,128]{1,0:T(8,128)S(1)}, u32[]{:S(2)}, u32[]{:S(2)}) %collective-permute-start.6) | collective-permute-done | bytes 69664 | tf_op jit(solution)/shard_map/ppermute | solution.py:331
  20.8 0.0 collective-permute-start.10
  20.8 3.7 %collective-permute-done.5.refs_2_ = f32[136,128]{1,0:T(8,128)S(1)} collective-permute-done((f32[136,128]{1,0:T(8,128)S(1)}, f32[136,128]{1,0:T(8,128)S(1)}, u32[]{:S(2)}, u32[]{:S(2)}) %collective-permute-start.5) | collective-permute-done | bytes 69664 | tf_op jit(solution)/shard_map/ppermute | solution.py:331
  24.5 0.0 collective-permute-start.9
  24.5 0.0 collective-permute-done.4.refs_1_
  24.5 0.5 %collective-permute-start.8 = (f32[136,128]{1,0:T(8,128)S(1)}, f32[136,128]{1,0:T(8,128)S(1)}, u32[]{:S(2)}, u32[]{:S(2)}) collective-permute-start(f32[136,128]{1,0:T(8,128)S(1)} %collective-permute-done.4.refs_1_), channel_id=1, source_target_pairs={{0,1},{1,0},{2,3},{3,2},{4,5},{5,4},{6,7},{7,6},{8,9},{9,8},{10,11... | collective-permute-start | bytes 208904 | tf_op jit(solution)/shard_map/ppermute | solution.py:331
  25.0 0.0 collective-permute-done.7.refs_4_
  25.0 0.0 collective-permute-done.10.refs_7_
  25.0 0.7 %collective-permute-done.9.refs_6_ = f32[136,128]{1,0:T(8,128)S(1)} collective-permute-done((f32[136,128]{1,0:T(8,128)S(1)}, f32[136,128]{1,0:T(8,128)S(1)}, u32[]{:S(2)}, u32[]{:S(2)}) %collective-permute-start.9) | collective-permute-done | bytes 69664 | tf_op jit(solution)/shard_map/ppermute | solution.py:331
  25.7 0.2 collective-permute-done.8.refs_5_
  25.9 0.0 copy-done.3
  25.9 3.6 %shard_map.115 = (f32[128,128]{1,0:T(8,128)}, f32[128,128]{1,0:T(8,128)}) custom-call(s32[4,64]{1,0:T(4,128)S(1)} %get-tuple-element.10.index_ref, s32[4,64]{1,0:T(4,128)S(1)} %bitcast.13, f32[136,128]{1,0:T(8,128)S(1)} %get-tuple-element.11.refs_0_, f32[136,128]{1,0:T(8,128)S(1)} %collective-permute-done.4.refs_1_, ...), custom_call_target="tpu_custom_call" | custom-call | tf_op jit(solution)/shard_map/pallas_call | solution.py:335
  (7 shorter events, 0.0 us)
Async XLA Ops:
  0.6 12.1 %copy-start.5 = (s32[1,64,4]{1,2,0:T(4,128)S(1)}, s32[1,64,4]{1,2,0:T(4,128)}, u32[]{:S(2)}) copy-start(s32[1,64,4]{1,2,0:T(4,128)} %param.16) | copy-start | bytes 3076
  0.6 12.1 %copy-start.4 = (s32[1,64,4]{1,2,0:T(4,128)S(1)}, s32[1,64,4]{1,2,0:T(4,128)}, u32[]{:S(2)}) copy-start(s32[1,64,4]{1,2,0:T(4,128)} %param.15) | copy-start | bytes 3076
  0.7 12.1 %copy-start.6 = (s32[1,64]{1,0:T(1,128)S(1)}, s32[1,64]{1,0:T(1,128)}, u32[]{:S(2)}) copy-start(s32[1,64]{1,0:T(1,128)} %flags_ref.1) | copy-start | bytes 772
  1.8 10.1 %collective-permute-start.1 = (f32[24,128]{1,0:T(8,128)S(1)}, f32[24,128]{1,0:T(8,128)S(1)}, u32[]{:S(2)}, u32[]{:S(2)}) collective-permute-start(f32[24,128]{1,0:T(8,128)S(1)} %get-tuple-element.8), channel_id=1, source_target_pairs={{0,0},{8,16},{16,8},{24,24},{1,1},{9,17},{17,9},{25,25},{2,2},{10,... | collective-permute-start | bytes 36872 | tf_op jit(solution)/shard_map/ppermute | solution.py:302
  2.5 9.4 %collective-permute-start = (f32[24,128]{1,0:T(8,128)S(1)}, f32[24,128]{1,0:T(8,128)S(1)}, u32[]{:S(2)}, u32[]{:S(2)}) collective-permute-start(f32[24,128]{1,0:T(8,128)S(1)} %get-tuple-element.8), channel_id=1, source_target_pairs={{0,8},{8,0},{16,24},{24,16},{1,9},{9,1},{17,25},{25,17},{2,10},{10... | collective-permute-start | bytes 36872 | tf_op jit(solution)/shard_map/ppermute | solution.py:303
  8.2 3.7 %collective-permute-start.3 = (f32[24,128]{1,0:T(8,128)S(1)}, f32[24,128]{1,0:T(8,128)S(1)}, u32[]{:S(2)}, u32[]{:S(2)}) collective-permute-start(f32[24,128]{1,0:T(8,128)S(1)} %get-tuple-element.9), channel_id=1, source_target_pairs={{0,0},{1,2},{2,1},{3,4},{4,3},{5,6},{6,5},{7,7},{8,8},{9,10},{10,9... | collective-permute-start | bytes 36872 | tf_op jit(solution)/shard_map/ppermute | solution.py:304
  8.9 3.8 %collective-permute-start.2 = (f32[24,128]{1,0:T(8,128)S(1)}, f32[24,128]{1,0:T(8,128)S(1)}, u32[]{:S(2)}, u32[]{:S(2)}) collective-permute-start(f32[24,128]{1,0:T(8,128)S(1)} %get-tuple-element.9), channel_id=1, source_target_pairs={{0,1},{1,0},{2,3},{3,2},{4,5},{5,4},{6,7},{7,6},{8,9},{9,8},{10,11... | collective-permute-start | bytes 36872 | tf_op jit(solution)/shard_map/ppermute | solution.py:305
  12.8 13.1 %copy-start = (f32[1,64,4,16,256]{4,3,2,1,0:T(8,128)S(1)}, f32[1,64,4,16,256]{4,3,2,1,0:T(8,128)}, u32[]{:S(2)}) copy-start(f32[1,64,4,16,256]{4,3,2,1,0:T(8,128)} %param.19) | copy-start | bytes 12582916
  12.8 13.1 %copy-start.1 = (f32[1,64,4,16,256]{4,3,2,1,0:T(8,128)S(1)}, f32[1,64,4,16,256]{4,3,2,1,0:T(8,128)}, u32[]{:S(2)}) copy-start(f32[1,64,4,16,256]{4,3,2,1,0:T(8,128)} %param.18) | copy-start | bytes 12582916
  12.8 13.1 %copy-start.2 = (f32[256,256]{1,0:T(8,128)S(1)}, f32[256,256]{1,0:T(8,128)}, u32[]{:S(2)}) copy-start(f32[256,256]{1,0:T(8,128)} %refs_8_.1) | copy-start | bytes 786436
  12.8 13.1 %copy-start.3 = (s32[1,64,4]{1,2,0:T(4,128)S(1)}, s32[1,64,4]{1,2,0:T(4,128)}, u32[]{:S(2)}) copy-start(s32[1,64,4]{1,2,0:T(4,128)} %param.17) | copy-start | bytes 3076
  14.2 6.6 %collective-permute-start.6 = (f32[136,128]{1,0:T(8,128)S(1)}, f32[136,128]{1,0:T(8,128)S(1)}, u32[]{:S(2)}, u32[]{:S(2)}) collective-permute-start(f32[136,128]{1,0:T(8,128)S(1)} %get-tuple-element.11.refs_0_), channel_id=1, source_target_pairs={{0,6},{1,7},{2,4},{3,5},{4,2},{5,3},{6,0},{7,1},{8,14},{9,15},{10,... | collective-permute-start | bytes 208904 | tf_op jit(solution)/shard_map/ppermute | solution.py:331
  18.4 6.1 %collective-permute-start.5 = (f32[136,128]{1,0:T(8,128)S(1)}, f32[136,128]{1,0:T(8,128)S(1)}, u32[]{:S(2)}, u32[]{:S(2)}) collective-permute-start(f32[136,128]{1,0:T(8,128)S(1)} %get-tuple-element.11.refs_0_), channel_id=1, source_target_pairs={{0,4},{1,5},{2,6},{3,7},{4,0},{5,1},{6,2},{7,3},{8,12},{9,13},{10,... | collective-permute-start | bytes 208904 | tf_op jit(solution)/shard_map/ppermute | solution.py:331
  18.4 6.1 %collective-permute-start.4 = (f32[136,128]{1,0:T(8,128)S(1)}, f32[136,128]{1,0:T(8,128)S(1)}, u32[]{:S(2)}, u32[]{:S(2)}) collective-permute-start(f32[136,128]{1,0:T(8,128)S(1)} %get-tuple-element.11.refs_0_), channel_id=1, source_target_pairs={{0,2},{1,3},{2,0},{3,1},{4,6},{5,7},{6,4},{7,5},{8,10},{9,11},{10,... | collective-permute-start | bytes 208904 | tf_op jit(solution)/shard_map/ppermute | solution.py:331
  19.0 6.0 %collective-permute-start.7 = (f32[136,128]{1,0:T(8,128)S(1)}, f32[136,128]{1,0:T(8,128)S(1)}, u32[]{:S(2)}, u32[]{:S(2)}) collective-permute-start(f32[136,128]{1,0:T(8,128)S(1)} %get-tuple-element.11.refs_0_), channel_id=1, source_target_pairs={{0,1},{1,0},{2,3},{3,2},{4,5},{5,4},{6,7},{7,6},{8,9},{9,8},{10,11... | collective-permute-start | bytes 208904 | tf_op jit(solution)/shard_map/ppermute | solution.py:331
  20.8 4.2 %collective-permute-start.10 = (f32[136,128]{1,0:T(8,128)S(1)}, f32[136,128]{1,0:T(8,128)S(1)}, u32[]{:S(2)}, u32[]{:S(2)}) collective-permute-start(f32[136,128]{1,0:T(8,128)S(1)} %collective-permute-done.6.refs_3_), channel_id=1, source_target_pairs={{0,1},{1,0},{2,3},{3,2},{4,5},{5,4},{6,7},{7,6},{8,9},{9,8},{10,11... | collective-permute-start | bytes 208904 | tf_op jit(solution)/shard_map/ppermute | solution.py:331
  24.5 1.3 %collective-permute-start.9 = (f32[136,128]{1,0:T(8,128)S(1)}, f32[136,128]{1,0:T(8,128)S(1)}, u32[]{:S(2)}, u32[]{:S(2)}) collective-permute-start(f32[136,128]{1,0:T(8,128)S(1)} %collective-permute-done.5.refs_2_), channel_id=1, source_target_pairs={{0,1},{1,0},{2,3},{3,2},{4,5},{5,4},{6,7},{7,6},{8,9},{9,8},{10,11... | collective-permute-start | bytes 208904 | tf_op jit(solution)/shard_map/ppermute | solution.py:331
  24.5 1.4 %collective-permute-start.8 = (f32[136,128]{1,0:T(8,128)S(1)}, f32[136,128]{1,0:T(8,128)S(1)}, u32[]{:S(2)}, u32[]{:S(2)}) collective-permute-start(f32[136,128]{1,0:T(8,128)S(1)} %collective-permute-done.4.refs_1_), channel_id=1, source_target_pairs={{0,1},{1,0},{2,3},{3,2},{4,5},{5,4},{6,7},{7,6},{8,9},{9,8},{10,11... | collective-permute-start | bytes 208904 | tf_op jit(solution)/shard_map/ppermute | solution.py:331

commit v3 on v2

--- a/solution.py
+++ b/solution.py
@@ -10,7 +10,7 @@
 
 TSIDE = 16
 PASSES = 3
-GROUP = 8
+GROUP = 64
 LANES = 128
 SUB = 8
 step_size = 0.1
@@ -57,7 +57,9 @@
     for d in (1, 2, 4):
         low_row, low_group = (sub & d) == 0, (group & d) == 0
         up = pltpu.roll(pltpu.roll(value, SUB - d, row_axis), TSIDE * d, lane_axis)
-        down = pltpu.roll(pltpu.roll(value, d, row_axis), LANES - TSIDE * d, lane_axis)
+        down = up
+        if d < 4:
+            down = pltpu.roll(pltpu.roll(value, d, row_axis), LANES - TSIDE * d, lane_axis)
         value = jnp.where(
             low_row == low_group, value, jnp.where(low_row, up, down)
         )
@@ -84,11 +86,74 @@
     return current
 
 
+def strip_picard(mains, strips, tail_inside, strip_inside):
+    tall = mains[0].shape[0]
+    lane = iota((SUB, LANES), 1)
+    sub = iota((SUB, LANES), 0)
+    groups = tall // SUB - 1
+
+    def clear(main):
+        tail = jnp.where(tail_inside, main[tall - SUB :], 0.0)
+        return jnp.concatenate([main[: tall - SUB], tail], axis=0)
+
+    def strip_shifts(value):
+        ahead, behind = pltpu.roll(value, SUB - 1, 0), pltpu.roll(value, 1, 0)
+        return (
+            jnp.where(sub == SUB - 1, pltpu.roll(ahead, LANES - 8, 1), ahead),
+            jnp.where(sub == 0, pltpu.roll(behind, 8, 1), behind),
+            pltpu.roll(value, LANES - 1, 1),
+            pltpu.roll(value, 1, 1),
+        )
+
+    def main_shifts(value, sides):
+        beyond = jnp.where(
+            lane % 8 == 1, pltpu.roll(sides[0], LANES - 1, 1), pltpu.roll(sides[1], LANES - 3, 1)
+        )
+        moved = [pltpu.roll(beyond, (LANES - 1 - 8 * g) % LANES, 1) for g in range(groups)]
+        moved = jnp.concatenate(moved + [jnp.zeros((SUB, LANES), jnp.float32)], axis=0)
+        at = iota(value.shape, 1)
+        return (
+            pltpu.roll(value, tall - 1, 0),
+            pltpu.roll(value, 1, 0),
+            jnp.where(at == LANES - 1, moved, pltpu.roll(value, LANES - 1, 1)),
+            jnp.where(at == 0, moved, pltpu.roll(value, 1, 1)),
+        )
+
+    def prepare(shifts, opening, pressure, inject, clear):
+        base = clear(opening + step_size * inject)
+        return base, [clear((other - pressure) * (step_size / 24.0)) for other in shifts]
+
+    def advance(shifts, cubed, base, slopes):
+        current = base
+        for other, slope in zip(shifts, slopes):
+            current = current + (cubed + other) * slope
+        return current
+
+    opening, pressure = clear(mains[0]), clear(mains[1])
+    clears = [lambda x, ok=ok: jnp.where(ok, x, 0.0) for ok in strip_inside]
+    sides = [[clears[i](strip[i]) for i in range(2)] for strip in strips]
+    base, slopes = prepare(main_shifts(pressure, sides[1]), opening, pressure, mains[2], clear)
+    edges = [
+        prepare(strip_shifts(sides[1][i]), sides[0][i], sides[1][i], sides[2][i], clears[i])
+        for i in range(2)
+    ]
+    current, beside = opening, sides[0]
+    for done in range(PASSES):
+        cubed = current * current * current
+        cubes = [value * value * value for value in beside]
+        current = advance(main_shifts(cubed, cubes), cubed, base, slopes)
+        if done < PASSES - 1:
+            beside = [
+                advance(strip_shifts(cube), cube, *edge) for cube, edge in zip(cubes, edges)
+            ]
+    return current
+
+
 def stencil_kernel(
     counts,
-    flag_ref,
     flags_ref,
     fields_ref,
+    edges_ref,
     rows_a_ref,
     rows_b_ref,
     cols_a_ref,
@@ -101,12 +166,11 @@
     n_row, n_col = counts
     rows, cols = fields_ref.shape[1:]
     old = [fields_ref.at[f] for f in range(3)]
-    wide, tall = cols + LANES, rows + SUB
     me_row, me_col = lax.axis_index("row"), lax.axis_index("col")
     row_even, col_even = me_row % 2 == 0, me_col % 2 == 0
     sub = iota((SUB, LANES), 0)
     lane = iota((SUB, LANES), 1)
-    fields, tails = [], []
+    mains, tails, strips = [], [], []
     for f, ref in enumerate(old):
         part = slice(f * SUB, (f + 1) * SUB)
         below = jnp.where(row_even, rows_a_ref[part, :], rows_b_ref[part, :])
@@ -114,21 +178,15 @@
         tail = jnp.where(sub < SUB // 2, below, above)
         right = jnp.where(col_even, cols_a_ref[part, :], cols_b_ref[part, :])
         left = jnp.where(col_even, cols_b_ref[part, :], cols_a_ref[part, :])
-        packed = jnp.where(lane % 8 < 3, left, right)
-        sides = []
-        for g in range(rows // SUB):
-            moved = pltpu.roll(packed, (LANES - 3 - 8 * g) % LANES, 1)
-            sides.append(jnp.where((lane < 3) | (lane >= LANES - 3), moved, 0.0))
-        sides.append(jnp.zeros((SUB, LANES), jnp.float32))
-        main = jnp.concatenate([ref[...], tail], axis=0)
-        fields.append(jnp.concatenate([main, jnp.concatenate(sides, axis=0)], axis=1))
+        mine = edges_ref[part, :]
+        mains.append(jnp.concatenate([ref[...], tail], axis=0))
         tails.append(tail)
-    row = iota((tall, wide), 0)
-    col = iota((tall, wide), 1)
-    row = me_row * rows + jnp.where(row < rows + SUB // 2, row, row - tall)
-    col = me_col * cols + jnp.where(col < cols + LANES // 2, col, col - wide)
-    inside = (row >= 0) & (row < n_row * rows) & (col >= 0) & (col < n_col * cols)
-    current = picard(*fields, inside)[:rows, :cols]
+        strips.append(
+            (jnp.where(lane % 8 < 3, left, mine), jnp.where(lane % 8 < 3, mine, right))
+        )
+    tail_inside = ((sub >= SUB // 2) | (me_row < n_row - 1)) & ((sub < SUB // 2) | (me_row > 0))
+    strip_inside = ((lane % 8 >= 3) | (me_col > 0), (lane % 8 < 3) | (me_col < n_col - 1))
+    current = strip_picard(mains, strips, tail_inside, strip_inside)[:rows]
     tiles = swap_groups(current.reshape(rows // SUB, SUB, LANES))
     count = flags_ref.shape[1]
     ones = jnp.where(iota((count, count), 0) == iota((count, count), 1), flags_ref[...], 0)
@@ -153,34 +211,75 @@
             )
     side = cols // TSIDE
     for at, tile in ((0, 0), (10, count - side), (69, side - 1), (79, count - 1)):
-        corner = jnp.where(
-            (lane >= at) & (lane < at + 5), flag_ref[0, tile].astype(jnp.float32), corner
-        )
+        mark = jnp.broadcast_to(flags[tile : tile + 1, :], (SUB, LANES))
+        corner = jnp.where((lane >= at) & (lane < at + 5), mark, corner)
     out_ref[2 * count :, :] = corner
     step = column_ref[...] ^ me_col
     index_ref[...] = ((step >> 1) + (step & 1) * (n_col // 2)) * count + tile_ref[...]
 
 
+def lay_out(lower, upper):
+    parts = [
+        half[at : at + SUB, :] for at in range(0, lower.shape[0], SUB) for half in (lower, upper)
+    ]
+    return swap_groups(jnp.stack(parts)).reshape(len(parts) * SUB, LANES)
+
+
+def split(value):
+    high = value.astype(jnp.bfloat16)
+    return high, (value - high.astype(jnp.float32)).astype(jnp.bfloat16)
+
+
 def split_dot(left, right):
     dims = (((1,), (1,)), ((), ()))
 
     def dot(a, b):
         return lax.dot_general(a, b, dims, preferred_element_type=jnp.float32)
 
-    left_high = left.astype(jnp.bfloat16)
-    left_low = (left - left_high.astype(jnp.float32)).astype(jnp.bfloat16)
-    right_high = right.astype(jnp.bfloat16)
-    right_low = (right - right_high.astype(jnp.float32)).astype(jnp.bfloat16)
-    return dot(left_high, right_high) + (dot(left_high, right_low) + dot(left_low, right_high))
+    return dot(left[0], right[0]) + (dot(left[0], right[1]) + dot(left[1], right[0]))
+
+
+def self_kernel_of(
+    block_ref,
+    self_ref,
+    index_ref,
+    rank_ref,
+    open_ref,
+    base_ref,
+    high_ref,
+    low_ref,
+    keep_ref,
+    index_out,
+    rank_out,
+    sems,
+):
+    copies = [
+        pltpu.make_async_copy(index_ref, index_out, sems.at[0]),
+        pltpu.make_async_copy(rank_ref, rank_out, sems.at[1]),
+    ]
+    for copy in copies:
+        copy.start()
+    ranks = keep_ref.shape[1]
+    for rank in range(ranks + 1):
+        keep_ref[rank] = (iota((ranks, LANES), 0) < rank).astype(jnp.float32)
+    count = base_ref.shape[0]
+    lower, upper = block_ref[0:count, :], block_ref[count : 2 * count, :]
+    open_ref[...] = lay_out(lower, upper)
+    parts = split(self_ref[...])
+    high_ref[...], low_ref[...] = parts
+    base_ref[...] = split_dot(split(jnp.concatenate([lower, upper], axis=1)), parts)
+    for copy in copies:
+        copy.wait()
 
 
 def pressure_kernel(counts, index_ref, rank_ref, *refs):
     n_row, n_col = counts
     blocks = refs[:n_col]
-    self_ref, right_ref, left_ref, open_out, press_out, band, base, press, around, fixes = refs[n_col:]
+    open_ref, base_ref, high_ref, low_ref, keep_ref, right_ref, left_ref = refs[n_col : n_col + 7]
+    open_out, press_out, band, press, around, fixes = refs[n_col + 7 :]
     me_row, me_col = lax.axis_index("row"), lax.axis_index("col")
     count = press.shape[1]
-    rows, cols = open_out.shape
+    rows, _ = open_out.shape
     sub = iota((SUB, LANES), 0)
     lane = iota((SUB, LANES), 1)
     steps = [2 * i for i in range(n_col // 2)] + [2 * i + 1 for i in range(n_col // 2)]
@@ -223,47 +322,58 @@
         bottom = ref[2 * count - SUB : 2 * count, :]
         bottom = patch(bottom, before, first, ((4, 15, 0, 112, 2), (3, 15, 0, 96, 1)))
         bottom = patch(bottom, after, final, ((4, 13, last, 126, 2), (3, 14, last, 111, 1)))
-        lower = jnp.concatenate([top, ref[SUB:count, :]], axis=0)
-        upper = jnp.concatenate([ref[count : 2 * count - SUB, :], bottom], axis=0)
-        band[0, slot * count : (slot + 1) * count, :] = lower
-        band[1, slot * count : (slot + 1) * count, :] = upper
+        start = slot * count
+        band[0, start : start + SUB, :] = top
+        band[0, start + SUB : start + count, :] = ref[SUB:count, :]
+        band[1, start : start + count - SUB, :] = ref[count : 2 * count - SUB, :]
+        band[1, start + count - SUB : start + count, :] = bottom
         if slot == 0:
-            own = (lower, upper)
-
-    def lay_out(lower, upper):
-        parts = [
-            half[SUB * a : SUB * a + SUB, :] for a in range(rows // TSIDE) for half in (lower, upper)
-        ]
-        return swap_groups(jnp.stack(parts)).reshape(rows, cols)
-
-    open_out[...] = lay_out(*own)
-    base[...] = split_dot(jnp.concatenate(own, axis=1), self_ref[...])
+            ends = swap_groups(jnp.stack([top, bottom]))
+            shift = jnp.concatenate([top - ref[0:SUB, :], bottom - ref[2 * count - SUB : 2 * count, :]])
+    open_out[0:SUB, :] = ends[0]
+    open_out[SUB : rows - SUB, :] = open_ref[SUB : rows - SUB, :]
+    open_out[rows - SUB :, :] = ends[1]
+    first_rows = iota((2 * SUB, LANES), 0) < SUB
+    shift = jnp.concatenate(
+        [jnp.where(first_rows, shift, 0.0), jnp.where(first_rows, 0.0, shift)], axis=1
+    )
+    moved = split_dot(split(shift), (high_ref[...], low_ref[...]))
 
     links, ranks = right_ref.shape[1], right_ref.shape[2]
-    depth = iota((ranks, LANES), 0)
+
+    def half(h):
+        return slice(h * LANES, (h + 1) * LANES)
+
+    def target(t):
+        total = [None, None]
+        for k in range(links):
+            at = index_ref[k, t]
+            product = sum(right_ref[t, k, :, half(h)] * band[h, pl.ds(at, 1), :] for h in range(2))
+            coefficient = jnp.sum(product, axis=1, keepdims=True)
+            coefficient = coefficient * keep_ref[rank_ref[k, t]]
+            for h in range(2):
+                term = left_ref[t, k, :, half(h)] * coefficient
+                for at in range(0, ranks, SUB):
+                    part = term[at : at + SUB, :]
+                    total[h] = part if total[h] is None else total[h] + part
+        for h in range(2):
+            press[h, pl.ds(t, 1), :] = jnp.sum(total[h], axis=0, keepdims=True)
 
     def targets(group, carry):
         for i in range(GROUP):
-            t = group * GROUP + i
-            total = [jnp.zeros((ranks, LANES), jnp.float32)] * 2
-            for k in range(links):
-                at = index_ref[k, t]
-                product = sum(
-                    right_ref[t, k, :, h * LANES : (h + 1) * LANES] * band[h, pl.ds(at, 1), :]
-                    for h in range(2)
-                )
-                coefficient = jnp.sum(product, axis=1, keepdims=True)
-                coefficient = jnp.where(depth < rank_ref[k, t], coefficient, 0.0)
-                total = [
-                    total[h] + left_ref[t, k, :, h * LANES : (h + 1) * LANES] * coefficient
-                    for h in range(2)
-                ]
-            for h in range(2):
-                press[h, pl.ds(t, 1), :] = jnp.sum(total[h], axis=0, keepdims=True)
+            target(group * GROUP + i)
         return carry
 
-    lax.fori_loop(0, count // GROUP, targets, 0)
-    press_out[...] = lay_out(*(press[h] + base[:, h * LANES : (h + 1) * LANES] for h in range(2)))
+    if GROUP == count:
+        for t in range(count):
+            target(t)
+    else:
+        lax.fori_loop(0, count // GROUP, targets, 0)
+    base = base_ref[...]
+    base = jnp.concatenate(
+        [base[:SUB] + moved[:SUB], base[SUB : count - SUB], base[count - SUB :] + moved[SUB:]]
+    )
+    press_out[...] = lay_out(*(press[h] + base[:, half(h)] for h in range(2)))
 
 
 def local(
@@ -299,8 +409,11 @@
         compiler_params=pltpu.CompilerParams(vmem_limit_bytes=4 << 20),
         cost_estimate=pl.CostEstimate(flops=4_000_000_000, transcendentals=0, bytes_accessed=30_000_000),
     )(*(pltpu.with_memory_space_constraint(x, pltpu.HBM) for x in (opening_old, pressure_old, injection)))
-    rows_b = lax.ppermute(edge_rows, "row", neighbour_pairs(n_row, 1))
     rows_a = lax.ppermute(edge_rows, "row", neighbour_pairs(n_row, 0))
+    if n_row == 4:
+        rows_b = lax.ppermute(rows_a, "row", [(i, i ^ 2) for i in range(n_row)])
+    else:
+        rows_b = lax.ppermute(edge_rows, "row", neighbour_pairs(n_row, 1))
     cols_b = lax.ppermute(edge_cols, "col", neighbour_pairs(n_col, 1))
     cols_a = lax.ppermute(edge_cols, "col", neighbour_pairs(n_col, 0))
     block, index = pl.pallas_call(
@@ -309,7 +422,7 @@
             pltpu.VMEM((2 * count + SUB, LANES), f32),
             pltpu.VMEM((links, count), jnp.int32),
         ],
-        in_specs=[smem] + [vmem] * 8,
+        in_specs=[vmem] * 9,
         out_specs=[vmem] * 2,
         compiler_params=pltpu.CompilerParams(vmem_limit_bytes=4 << 20),
         cost_estimate=pl.CostEstimate(
@@ -317,8 +430,8 @@
         ),
     )(
         front_flags,
-        front_flags,
         held(fields),
+        held(edge_cols),
         held(rows_a),
         held(rows_b),
         held(cols_a),
@@ -332,24 +445,40 @@
 
     near = [block] + [exchange(block, step) for step in range(2, n_col, 2)]
     far = [exchange(value, 1) for value in near]
+    size, ranks = self_kernel.shape, left_factor.shape[3]
+    *own, index, rank = pl.pallas_call(
+        self_kernel_of,
+        out_shape=[
+            pltpu.VMEM((rows, cols), f32),
+            pltpu.VMEM((count, size[0]), f32),
+            pltpu.VMEM(size, jnp.bfloat16),
+            pltpu.VMEM(size, jnp.bfloat16),
+            pltpu.VMEM((ranks + 1, ranks, LANES), f32),
+            pltpu.SMEM((links, count), jnp.int32),
+            pltpu.SMEM((links, count), jnp.int32),
+        ],
+        in_specs=[vmem] * 4,
+        out_specs=[vmem] * 5 + [smem] * 2,
+        scratch_shapes=[pltpu.SemaphoreType.DMA((2,))],
+        compiler_params=pltpu.CompilerParams(vmem_limit_bytes=4 << 20),
+    )(held(block), self_kernel, held(index), source_rank[0].T)
     opening_new, pressure_new = pl.pallas_call(
         functools.partial(pressure_kernel, counts),
         out_shape=[jax.ShapeDtypeStruct((rows, cols), f32)] * 2,
-        in_specs=[smem] * 2 + [vmem] * (n_col + 3),
+        in_specs=[smem] * 2 + [vmem] * (n_col + 7),
         out_specs=[vmem] * 2,
         scratch_shapes=[
             pltpu.VMEM((2, n_col * count, LANES), f32),
-            pltpu.VMEM((count, 2 * LANES), f32),
             pltpu.VMEM((2, count, LANES), f32),
             pltpu.VMEM((n_col * SUB, LANES), f32),
             pltpu.VMEM((n_col * SUB, LANES), f32),
         ],
         compiler_params=pltpu.CompilerParams(vmem_limit_bytes=8 << 20),
     )(
-        index,
-        source_rank[0].T,
+        pltpu.with_memory_space_constraint(index, pltpu.SMEM),
+        pltpu.with_memory_space_constraint(rank, pltpu.SMEM),
         *(held(value) for value in near + far),
-        self_kernel,
+        *(held(value) for value in own),
         right_factor[0],
         left_factor[0],
     )

time: 29.6 us -> 26.1 us (0.88)
  starting transfers between devices: 15.4 us -> 13.2 us
  Pallas kernels: 6.08 us -> 4.87 us
    ppermute x1, starting transfers between devices: 5.77 us -> 3.03 us  [local(): rows_a = lax.ppermute(edge_rows, 'row', neighbour_pairs(n_row, 0))]
    ppermute x1, waiting for transfers between devices: 0.01 us -> 2.17 us  [local(): rows_b = lax.ppermute(rows_a, 'row', [(i, i ^ 2) for i in range(n_row)])]
    ppermute x7, waiting for transfers between devices: 6.35 us -> 4.9 us  [exchange(): return lax.ppermute(value, 'col', [(i, i ^ step) for i in range(n_col)])]
    pallas_call x1, Pallas kernels: 3.57 us -> 2.36 us  [local(): pl.pallas_call(functools.partial(pressure_kernel, counts), out_shape=[jax...]
    ppermute x1, starting transfers between devices: 0.66 us -> 1.52 us  [local(): rows_b = lax.ppermute(rows_a, 'row', [(i, i ^ 2) for i in range(n_row)])]
    ppermute x1, waiting for transfers between devices: 0.82 us -> 0.01 us  [local(): cols_a = lax.ppermute(edge_cols, 'col', neighbour_pairs(n_col, 0))]
    pallas_call x1, Pallas kernels: 1.37 us -> 0.74 us  [local(): pl.pallas_call(functools.partial(stencil_kernel, counts), out_shape=[pltp...]
    pallas_call x0 -> x1, Pallas kernels: none -> 0.63 us  [local(): pl.pallas_call(self_kernel_of, out_shape=[pltpu.VMEM((rows, cols), f32),...]
  transfers between devices with their start and end apart: 11 -> 11, of which waited for: 5 -> 5; matrix products, arithmetic and copies ran while one was open for 0% -> 0% of each run, Pallas kernels for 0% -> 2%
where the time goes in v3:
time: 26.1 us; the launch traced here: 25.9 us
  starting transfers between devices  13.2 us (51%)
  waiting for transfers between devices  7.08 us (27%)
  Pallas kernels  4.87 us (19%)
  between operations  0.75 us (3%)
    ppermute x7, starting transfers between devices, exchange(): return lax.ppermute(value, 'col', [(i, i ^ step) for i in range(n_col)])  4.97 us
    ppermute x7, waiting for transfers between devices, exchange(): return lax.ppermute(value, 'col', [(i, i ^ step) for i in range(n_col)])  4.9 us
    ppermute x1, starting transfers between devices, local(): rows_a = lax.ppermute(edge_rows, 'row', neighbour_pairs(n_row, 0))  3.03 us
    ppermute x1, starting transfers between devices, local(): cols_a = lax.ppermute(edge_cols, 'col', neighbour_pairs(n_col, 0))  3 us
    pallas_call x1, Pallas kernels, local(): pl.pallas_call(functools.partial(pressure_kernel, counts), out_shape=[jax...  2.36 us
    ppermute x1, waiting for transfers between devices, local(): rows_b = lax.ppermute(rows_a, 'row', [(i, i ^ 2) for i in range(n_row)])  2.17 us
    ppermute x1, starting transfers between devices, local(): rows_b = lax.ppermute(rows_a, 'row', [(i, i ^ 2) for i in range(n_row)])  1.52 us
    pallas_call x1, Pallas kernels, local(): pl.pallas_call(edges_kernel, out_shape=[pltpu.VMEM((3, rows, cols), f32)]...  1.14 us
  transfers between devices with their start and end apart: 11, of which 5 were waited for; matrix products, arithmetic and copies ran while one was open for 0% of the time, Pallas kernels for 2%

profile of v3, /device:TPU:0, one launch (start us, length us, event | category | flops | bytes accessed | tf_op | source)
XLA Modules:
  0.0 25.9 jit_solution(1979775522408950606)
XLA Ops:
  0.7 1.1 %shard_map.113 = (f32[3,128,128]{2,1,0:T(8,128)S(1)}, f32[24,128]{1,0:T(8,128)S(1)}, f32[24,128]{1,0:T(8,128)S(1)}) custom-call(f32[128,128]{1,0:T(8,128)} %open_ref.1, f32[128,128]{1,0:T(8,128)} %press_ref.1, f32[128,128]{1,0:T(8,128)} %inject_ref.1), custom_call_target="tpu_custom_call" | custom-call | flops 4000000000 | bytes 30000000 | tf_op jit(solution)/shard_map/pallas_call | solution.py:403
  1.8 3.0 %collective-permute-start = (f32[24,128]{1,0:T(8,128)S(1)}, f32[24,128]{1,0:T(8,128)S(1)}, u32[]{:S(2)}, u32[]{:S(2)}) collective-permute-start(f32[24,128]{1,0:T(8,128)S(1)} %get-tuple-element.16), channel_id=1, source_target_pairs={{0,8},{8,0},{16,24},{24,16},{1,9},{9,1},{17,25},{25,17},{2,10},{10... | collective-permute-start | bytes 36872 | tf_op jit(solution)/shard_map/ppermute | solution.py:412
  4.8 0.7 %collective-permute-start.3 = (f32[24,128]{1,0:T(8,128)S(1)}, f32[24,128]{1,0:T(8,128)S(1)}, u32[]{:S(2)}, u32[]{:S(2)}) collective-permute-start(f32[24,128]{1,0:T(8,128)S(1)} %get-tuple-element.15.edges_ref), channel_id=1, source_target_pairs={{0,0},{1,2},{2,1},{3,4},{4,3},{5,6},{6,5},{7,7},{8,8},{9,10},{10,9... | collective-permute-start | bytes 36872 | tf_op jit(solution)/shard_map/ppermute | solution.py:417
  5.5 3.0 %collective-permute-start.2 = (f32[24,128]{1,0:T(8,128)S(1)}, f32[24,128]{1,0:T(8,128)S(1)}, u32[]{:S(2)}, u32[]{:S(2)}) collective-permute-start(f32[24,128]{1,0:T(8,128)S(1)} %get-tuple-element.15.edges_ref), channel_id=1, source_target_pairs={{0,1},{1,0},{2,3},{3,2},{4,5},{5,4},{6,7},{7,6},{8,9},{9,8},{10,11... | collective-permute-start | bytes 36872 | tf_op jit(solution)/shard_map/ppermute | solution.py:418
  8.5 0.0 collective-permute-done.rows_a_ref
  8.5 1.5 %collective-permute-start.1 = (f32[24,128]{1,0:T(8,128)S(1)}, f32[24,128]{1,0:T(8,128)S(1)}, u32[]{:S(2)}, u32[]{:S(2)}) collective-permute-start(f32[24,128]{1,0:T(8,128)S(1)} %collective-permute-done.rows_a_ref), channel_id=1, source_target_pairs={{0,16},{8,24},{16,0},{24,8},{1,17},{9,25},{17,1},{25,9},{2,18},{10... | collective-permute-start | bytes 36872 | tf_op jit(solution)/shard_map/ppermute | solution.py:414
  10.0 0.0 collective-permute-done.3.cols_b_ref
  10.0 0.0 collective-permute-done.2.cols_a_ref
  10.0 2.2 %collective-permute-done.1.rows_b_ref = f32[24,128]{1,0:T(8,128)S(1)} collective-permute-done((f32[24,128]{1,0:T(8,128)S(1)}, f32[24,128]{1,0:T(8,128)S(1)}, u32[]{:S(2)}, u32[]{:S(2)}) %collective-permute-start.1) | collective-permute-done | bytes 12320 | tf_op jit(solution)/shard_map/ppermute | solution.py:414
  12.2 0.0 copy-done.5
  12.2 0.0 copy-start.2
  12.2 0.0 copy-start.3
  12.2 0.0 copy-start
  12.2 0.0 copy-start.1
  12.3 0.7 %shard_map.114 = (f32[136,128]{1,0:T(8,128)S(1)}, s32[4,64]{1,0:T(4,128)S(1)}) custom-call(s32[1,64]{1,0:T(1,128)S(1)} %copy-done.6, f32[3,128,128]{2,1,0:T(8,128)S(1)} %get-tuple-element.14.fields_ref, f32[24,128]{1,0:T(8,128)S(1)} %get-tuple-element.15.edges_ref, f32[24,128]{1,0:T(8,128)S(1)} %collective-permute-done.rows_a_ref, ...), custom_call_target="tpu_custom_call" | custom-call | flops 4000000000 | bytes 30000000 | tf_op jit(solution)/shard_map/pallas_call | solution.py:419
  13.0 2.2 %collective-permute-start.6 = (f32[136,128]{1,0:T(8,128)S(1)}, f32[136,128]{1,0:T(8,128)S(1)}, u32[]{:S(2)}, u32[]{:S(2)}) collective-permute-start(f32[136,128]{1,0:T(8,128)S(1)} %get-tuple-element.17.block_ref.refs_0_), channel_id=1, source_target_pairs={{0,6},{1,7},{2,4},{3,5},{4,2},{5,3},{6,0},{7,1},{8,14},{9,15},{10,... | collective-permute-start | bytes 208904 | tf_op jit(solution)/shard_map/ppermute | solution.py:444
  15.2 0.9 %collective-permute-start.5 = (f32[136,128]{1,0:T(8,128)S(1)}, f32[136,128]{1,0:T(8,128)S(1)}, u32[]{:S(2)}, u32[]{:S(2)}) collective-permute-start(f32[136,128]{1,0:T(8,128)S(1)} %get-tuple-element.17.block_ref.refs_0_), channel_id=1, source_target_pairs={{0,4},{1,5},{2,6},{3,7},{4,0},{5,1},{6,2},{7,3},{8,12},{9,13},{10,... | collective-permute-start | bytes 208904 | tf_op jit(solution)/shard_map/ppermute | solution.py:444
  16.1 1.3 %collective-permute-start.4 = (f32[136,128]{1,0:T(8,128)S(1)}, f32[136,128]{1,0:T(8,128)S(1)}, u32[]{:S(2)}, u32[]{:S(2)}) collective-permute-start(f32[136,128]{1,0:T(8,128)S(1)} %get-tuple-element.17.block_ref.refs_0_), channel_id=1, source_target_pairs={{0,2},{1,3},{2,0},{3,1},{4,6},{5,7},{6,4},{7,5},{8,10},{9,11},{10,... | collective-permute-start | bytes 208904 | tf_op jit(solution)/shard_map/ppermute | solution.py:444
  17.5 0.0 collective-permute-start.7
  17.5 2.5 %collective-permute-done.6.refs_3_ = f32[136,128]{1,0:T(8,128)S(1)} collective-permute-done((f32[136,128]{1,0:T(8,128)S(1)}, f32[136,128]{1,0:T(8,128)S(1)}, u32[]{:S(2)}, u32[]{:S(2)}) %collective-permute-start.6) | collective-permute-done | bytes 69664 | tf_op jit(solution)/shard_map/ppermute | solution.py:444
  19.9 0.0 collective-permute-start.10
  19.9 2.2 %collective-permute-done.5.refs_2_ = f32[136,128]{1,0:T(8,128)S(1)} collective-permute-done((f32[136,128]{1,0:T(8,128)S(1)}, f32[136,128]{1,0:T(8,128)S(1)}, u32[]{:S(2)}, u32[]{:S(2)}) %collective-permute-start.5) | collective-permute-done | bytes 69664 | tf_op jit(solution)/shard_map/ppermute | solution.py:444
  22.1 0.0 collective-permute-start.9
  22.1 0.0 collective-permute-done.4.refs_1_
  22.1 0.5 %collective-permute-start.8 = (f32[136,128]{1,0:T(8,128)S(1)}, f32[136,128]{1,0:T(8,128)S(1)}, u32[]{:S(2)}, u32[]{:S(2)}) collective-permute-start(f32[136,128]{1,0:T(8,128)S(1)} %collective-permute-done.4.refs_1_), channel_id=1, source_target_pairs={{0,1},{1,0},{2,3},{3,2},{4,5},{5,4},{6,7},{7,6},{8,9},{9,8},{10,11... | collective-permute-start | bytes 208904 | tf_op jit(solution)/shard_map/ppermute | solution.py:444
  22.6 0.0 copy-done.2
  22.6 0.6 %shard_map.115 = (f32[128,128]{1,0:T(8,128)S(1)}, f32[64,256]{1,0:T(8,128)S(1)}, bf16[256,256]{1,0:T(8,128)(2,1)S(1)}, bf16[256,256]{1,0:T(8,128)(2,1)S(1)}, f32...) custom-call(f32[136,128]{1,0:T(8,128)S(1)} %get-tuple-element.17.block_ref.refs_0_, ...), custom_call_target="tpu_custom_call" | custom-call | tf_op jit(solution)/shard_map/pallas_call | solution.py:449
  23.3 0.0 collective-permute-done.7.refs_4_
  23.3 0.0 collective-permute-done.10.refs_7_
  23.3 0.1 collective-permute-done.9.refs_6_
  23.4 0.2 collective-permute-done.8.refs_5_
  23.5 2.4 %shard_map.116 = (f32[128,128]{1,0:T(8,128)}, f32[128,128]{1,0:T(8,128)}) custom-call(s32[4,64]{1,0:T(4,128)S(4)} %get-tuple-element.19.index_ref, s32[4,64]{1,0:T(4,128)S(4)} %get-tuple-element.20.rank_ref, f32[136,128]{1,0:T(8,128)S(1)} %get-tuple-element.17.block_ref.refs_0_, f32[136,128]{1,0:T(8,128)S(1)} %collective-permute-done.4.refs_1_, ...), custom_call_target="tpu_custom_call" | custom-call | tf_op jit(solution)/shard_map/pallas_call | solution.py:465
  (8 shorter events, 0.0 us)
Async XLA Ops:
  0.6 11.6 %copy-start.5 = (s32[1,64,4]{1,2,0:T(4,128)S(1)}, s32[1,64,4]{1,2,0:T(4,128)}, u32[]{:S(2)}) copy-start(s32[1,64,4]{1,2,0:T(4,128)} %param.16) | copy-start | bytes 3076
  0.6 11.6 %copy-start.4 = (s32[1,64,4]{1,2,0:T(4,128)S(1)}, s32[1,64,4]{1,2,0:T(4,128)}, u32[]{:S(2)}) copy-start(s32[1,64,4]{1,2,0:T(4,128)} %param.15) | copy-start | bytes 3076
  0.7 11.6 %copy-start.6 = (s32[1,64]{1,0:T(1,128)S(1)}, s32[1,64]{1,0:T(1,128)}, u32[]{:S(2)}) copy-start(s32[1,64]{1,0:T(1,128)} %flags_ref.1) | copy-start | bytes 772
  1.8 6.7 %collective-permute-start = (f32[24,128]{1,0:T(8,128)S(1)}, f32[24,128]{1,0:T(8,128)S(1)}, u32[]{:S(2)}, u32[]{:S(2)}) collective-permute-start(f32[24,128]{1,0:T(8,128)S(1)} %get-tuple-element.16), channel_id=1, source_target_pairs={{0,8},{8,0},{16,24},{24,16},{1,9},{9,1},{17,25},{25,17},{2,10},{10... | collective-permute-start | bytes 36872 | tf_op jit(solution)/shard_map/ppermute | solution.py:412
  4.8 5.2 %collective-permute-start.3 = (f32[24,128]{1,0:T(8,128)S(1)}, f32[24,128]{1,0:T(8,128)S(1)}, u32[]{:S(2)}, u32[]{:S(2)}) collective-permute-start(f32[24,128]{1,0:T(8,128)S(1)} %get-tuple-element.15.edges_ref), channel_id=1, source_target_pairs={{0,0},{1,2},{2,1},{3,4},{4,3},{5,6},{6,5},{7,7},{8,8},{9,10},{10,9... | collective-permute-start | bytes 36872 | tf_op jit(solution)/shard_map/ppermute | solution.py:417
  5.5 4.5 %collective-permute-start.2 = (f32[24,128]{1,0:T(8,128)S(1)}, f32[24,128]{1,0:T(8,128)S(1)}, u32[]{:S(2)}, u32[]{:S(2)}) collective-permute-start(f32[24,128]{1,0:T(8,128)S(1)} %get-tuple-element.15.edges_ref), channel_id=1, source_target_pairs={{0,1},{1,0},{2,3},{3,2},{4,5},{5,4},{6,7},{7,6},{8,9},{9,8},{10,11... | collective-permute-start | bytes 36872 | tf_op jit(solution)/shard_map/ppermute | solution.py:418
  8.5 3.7 %collective-permute-start.1 = (f32[24,128]{1,0:T(8,128)S(1)}, f32[24,128]{1,0:T(8,128)S(1)}, u32[]{:S(2)}, u32[]{:S(2)}) collective-permute-start(f32[24,128]{1,0:T(8,128)S(1)} %collective-permute-done.rows_a_ref), channel_id=1, source_target_pairs={{0,16},{8,24},{16,0},{24,8},{1,17},{9,25},{17,1},{25,9},{2,18},{10... | collective-permute-start | bytes 36872 | tf_op jit(solution)/shard_map/ppermute | solution.py:414
  12.2 10.4 %copy-start.2 = (f32[256,256]{1,0:T(8,128)S(1)}, f32[256,256]{1,0:T(8,128)}, u32[]{:S(2)}) copy-start(f32[256,256]{1,0:T(8,128)} %self_ref.1) | copy-start | bytes 786436
  12.2 10.4 %copy-start.3 = (s32[1,64,4]{1,2,0:T(4,128)S(1)}, s32[1,64,4]{1,2,0:T(4,128)}, u32[]{:S(2)}) copy-start(s32[1,64,4]{1,2,0:T(4,128)} %param.17) | copy-start | bytes 3076
  12.2 11.3 %copy-start = (f32[1,64,4,16,256]{4,3,2,1,0:T(8,128)S(1)}, f32[1,64,4,16,256]{4,3,2,1,0:T(8,128)}, u32[]{:S(2)}) copy-start(f32[1,64,4,16,256]{4,3,2,1,0:T(8,128)} %param.19) | copy-start | bytes 12582916
  12.2 11.3 %copy-start.1 = (f32[1,64,4,16,256]{4,3,2,1,0:T(8,128)S(1)}, f32[1,64,4,16,256]{4,3,2,1,0:T(8,128)}, u32[]{:S(2)}) copy-start(f32[1,64,4,16,256]{4,3,2,1,0:T(8,128)} %param.18) | copy-start | bytes 12582916
  13.0 6.9 %collective-permute-start.6 = (f32[136,128]{1,0:T(8,128)S(1)}, f32[136,128]{1,0:T(8,128)S(1)}, u32[]{:S(2)}, u32[]{:S(2)}) collective-permute-start(f32[136,128]{1,0:T(8,128)S(1)} %get-tuple-element.17.block_ref.refs_0_), channel_id=1, source_target_pairs={{0,6},{1,7},{2,4},{3,5},{4,2},{5,3},{6,0},{7,1},{8,14},{9,15},{10,... | collective-permute-start | bytes 208904 | tf_op jit(solution)/shard_map/ppermute | solution.py:444
  15.2 6.9 %collective-permute-start.5 = (f32[136,128]{1,0:T(8,128)S(1)}, f32[136,128]{1,0:T(8,128)S(1)}, u32[]{:S(2)}, u32[]{:S(2)}) collective-permute-start(f32[136,128]{1,0:T(8,128)S(1)} %get-tuple-element.17.block_ref.refs_0_), channel_id=1, source_target_pairs={{0,4},{1,5},{2,6},{3,7},{4,0},{5,1},{6,2},{7,3},{8,12},{9,13},{10,... | collective-permute-start | bytes 208904 | tf_op jit(solution)/shard_map/ppermute | solution.py:444
  16.1 6.0 %collective-permute-start.4 = (f32[136,128]{1,0:T(8,128)S(1)}, f32[136,128]{1,0:T(8,128)S(1)}, u32[]{:S(2)}, u32[]{:S(2)}) collective-permute-start(f32[136,128]{1,0:T(8,128)S(1)} %get-tuple-element.17.block_ref.refs_0_), channel_id=1, source_target_pairs={{0,2},{1,3},{2,0},{3,1},{4,6},{5,7},{6,4},{7,5},{8,10},{9,11},{10,... | collective-permute-start | bytes 208904 | tf_op jit(solution)/shard_map/ppermute | solution.py:444
  17.5 5.8 %collective-permute-start.7 = (f32[136,128]{1,0:T(8,128)S(1)}, f32[136,128]{1,0:T(8,128)S(1)}, u32[]{:S(2)}, u32[]{:S(2)}) collective-permute-start(f32[136,128]{1,0:T(8,128)S(1)} %get-tuple-element.17.block_ref.refs_0_), channel_id=1, source_target_pairs={{0,1},{1,0},{2,3},{3,2},{4,5},{5,4},{6,7},{7,6},{8,9},{9,8},{10,11... | collective-permute-start | bytes 208904 | tf_op jit(solution)/shard_map/ppermute | solution.py:444
  19.9 3.4 %collective-permute-start.10 = (f32[136,128]{1,0:T(8,128)S(1)}, f32[136,128]{1,0:T(8,128)S(1)}, u32[]{:S(2)}, u32[]{:S(2)}) collective-permute-start(f32[136,128]{1,0:T(8,128)S(1)} %collective-permute-done.6.refs_3_), channel_id=1, source_target_pairs={{0,1},{1,0},{2,3},{3,2},{4,5},{5,4},{6,7},{7,6},{8,9},{9,8},{10,11... | collective-permute-start | bytes 208904 | tf_op jit(solution)/shard_map/ppermute | solution.py:444
  22.1 1.3 %collective-permute-start.9 = (f32[136,128]{1,0:T(8,128)S(1)}, f32[136,128]{1,0:T(8,128)S(1)}, u32[]{:S(2)}, u32[]{:S(2)}) collective-permute-start(f32[136,128]{1,0:T(8,128)S(1)} %collective-permute-done.5.refs_2_), channel_id=1, source_target_pairs={{0,1},{1,0},{2,3},{3,2},{4,5},{5,4},{6,7},{7,6},{8,9},{9,8},{10,11... | collective-permute-start | bytes 208904 | tf_op jit(solution)/shard_map/ppermute | solution.py:444
  22.1 1.4 %collective-permute-start.8 = (f32[136,128]{1,0:T(8,128)S(1)}, f32[136,128]{1,0:T(8,128)S(1)}, u32[]{:S(2)}, u32[]{:S(2)}) collective-permute-start(f32[136,128]{1,0:T(8,128)S(1)} %collective-permute-done.4.refs_1_), channel_id=1, source_target_pairs={{0,1},{1,0},{2,3},{3,2},{4,5},{5,4},{6,7},{7,6},{8,9},{9,8},{10,11... | collective-permute-start | bytes 208904 | tf_op jit(solution)/shard_map/ppermute | solution.py:444

commit v4 on v3

--- a/solution.py
+++ b/solution.py
@@ -80,9 +80,10 @@
     current = opening
     for _ in range(PASSES):
         cubed = current * current * current
-        current = base
-        for (a, s), slope in zip(shifts, slopes):
-            current = current + (cubed + pltpu.roll(cubed, s, a)) * slope
+        terms = [
+            (cubed + pltpu.roll(cubed, s, a)) * slope for (a, s), slope in zip(shifts, slopes)
+        ]
+        current = (base + terms[0]) + (terms[1] + (terms[2] + terms[3]))
     return current
 
 
@@ -124,10 +125,8 @@
         return base, [clear((other - pressure) * (step_size / 24.0)) for other in shifts]
 
     def advance(shifts, cubed, base, slopes):
-        current = base
-        for other, slope in zip(shifts, slopes):
-            current = current + (cubed + other) * slope
-        return current
+        terms = [(cubed + other) * slope for other, slope in zip(shifts, slopes)]
+        return (base + terms[0]) + (terms[1] + (terms[2] + terms[3]))
 
     opening, pressure = clear(mains[0]), clear(mains[1])
     clears = [lambda x, ok=ok: jnp.where(ok, x, 0.0) for ok in strip_inside]
@@ -225,18 +224,24 @@
     return swap_groups(jnp.stack(parts)).reshape(len(parts) * SUB, LANES)
 
 
-def split(value):
-    high = value.astype(jnp.bfloat16)
-    return high, (value - high.astype(jnp.float32)).astype(jnp.bfloat16)
+def split(value, parts=2):
+    pieces = []
+    for _ in range(parts):
+        pieces.append(value.astype(jnp.bfloat16))
+        value = value - pieces[-1].astype(jnp.float32)
+    return pieces
 
 
 def split_dot(left, right):
     dims = (((1,), (1,)), ((), ()))
-
-    def dot(a, b):
-        return lax.dot_general(a, b, dims, preferred_element_type=jnp.float32)
-
-    return dot(left[0], right[0]) + (dot(left[0], right[1]) + dot(left[1], right[0]))
+    total = None
+    for order in reversed(range(len(left))):
+        for i in range(order + 1):
+            term = lax.dot_general(
+                left[i], right[order - i], dims, preferred_element_type=jnp.float32
+            )
+            total = term if total is None else total + term
+    return total
 
 
 def self_kernel_of(
@@ -265,9 +270,9 @@
     count = base_ref.shape[0]
     lower, upper = block_ref[0:count, :], block_ref[count : 2 * count, :]
     open_ref[...] = lay_out(lower, upper)
-    parts = split(self_ref[...])
-    high_ref[...], low_ref[...] = parts
-    base_ref[...] = split_dot(split(jnp.concatenate([lower, upper], axis=1)), parts)
+    parts = split(self_ref[...], 3)
+    high_ref[...], low_ref[...] = parts[:2]
+    base_ref[...] = split_dot(split(jnp.concatenate([lower, upper], axis=1), 3), parts)
     for copy in copies:
         copy.wait()
 

time: 26.1 us -> 26.1 us (level)
  no operation moved by 1% of the time
where the time goes in v4:
time: 26.1 us; the launch traced here: 25.9 us
  starting transfers between devices  13.2 us (51%)
  waiting for transfers between devices  7.1 us (27%)
  Pallas kernels  4.89 us (19%)
  between operations  0.75 us (3%)
    ppermute x7, starting transfers between devices, exchange(): return lax.ppermute(value, 'col', [(i, i ^ step) for i in range(n_col)])  4.97 us
    ppermute x7, waiting for transfers between devices, exchange(): return lax.ppermute(value, 'col', [(i, i ^ step) for i in range(n_col)])  4.92 us
    ppermute x1, starting transfers between devices, local(): rows_a = lax.ppermute(edge_rows, 'row', neighbour_pairs(n_row, 0))  3.03 us
    ppermute x1, starting transfers between devices, local(): cols_a = lax.ppermute(edge_cols, 'col', neighbour_pairs(n_col, 0))  3 us
    pallas_call x1, Pallas kernels, local(): pl.pallas_call(functools.partial(pressure_kernel, counts), out_shape=[jax...  2.37 us
    ppermute x1, waiting for transfers between devices, local(): rows_b = lax.ppermute(rows_a, 'row', [(i, i ^ 2) for i in range(n_row)])  2.17 us
    ppermute x1, starting transfers between devices, local(): rows_b = lax.ppermute(rows_a, 'row', [(i, i ^ 2) for i in range(n_row)])  1.52 us
    pallas_call x1, Pallas kernels, local(): pl.pallas_call(edges_kernel, out_shape=[pltpu.VMEM((3, rows, cols), f32)]...  1.14 us
  transfers between devices with their start and end apart: 11, of which 5 were waited for; matrix products, arithmetic and copies ran while one was open for 0% of the time, Pallas kernels for 2%

profile of v4, /device:TPU:0, one launch (start us, length us, event | category | flops | bytes accessed | tf_op | source)
XLA Modules:
  0.0 25.9 jit_solution(3497479390988478356)
XLA Ops:
  0.7 1.1 %shard_map.113 = (f32[3,128,128]{2,1,0:T(8,128)S(1)}, f32[24,128]{1,0:T(8,128)S(1)}, f32[24,128]{1,0:T(8,128)S(1)}) custom-call(f32[128,128]{1,0:T(8,128)} %open_ref.1, f32[128,128]{1,0:T(8,128)} %press_ref.1, f32[128,128]{1,0:T(8,128)} %inject_ref.1), custom_call_target="tpu_custom_call" | custom-call | flops 4000000000 | bytes 30000000 | tf_op jit(solution)/shard_map/pallas_call | solution.py:408
  1.8 3.0 %collective-permute-start = (f32[24,128]{1,0:T(8,128)S(1)}, f32[24,128]{1,0:T(8,128)S(1)}, u32[]{:S(2)}, u32[]{:S(2)}) collective-permute-start(f32[24,128]{1,0:T(8,128)S(1)} %get-tuple-element.16), channel_id=1, source_target_pairs={{0,8},{8,0},{16,24},{24,16},{1,9},{9,1},{17,25},{25,17},{2,10},{10... | collective-permute-start | bytes 36872 | tf_op jit(solution)/shard_map/ppermute | solution.py:417
  4.8 0.7 %collective-permute-start.3 = (f32[24,128]{1,0:T(8,128)S(1)}, f32[24,128]{1,0:T(8,128)S(1)}, u32[]{:S(2)}, u32[]{:S(2)}) collective-permute-start(f32[24,128]{1,0:T(8,128)S(1)} %get-tuple-element.15.edges_ref), channel_id=1, source_target_pairs={{0,0},{1,2},{2,1},{3,4},{4,3},{5,6},{6,5},{7,7},{8,8},{9,10},{10,9... | collective-permute-start | bytes 36872 | tf_op jit(solution)/shard_map/ppermute | solution.py:422
  5.5 3.0 %collective-permute-start.2 = (f32[24,128]{1,0:T(8,128)S(1)}, f32[24,128]{1,0:T(8,128)S(1)}, u32[]{:S(2)}, u32[]{:S(2)}) collective-permute-start(f32[24,128]{1,0:T(8,128)S(1)} %get-tuple-element.15.edges_ref), channel_id=1, source_target_pairs={{0,1},{1,0},{2,3},{3,2},{4,5},{5,4},{6,7},{7,6},{8,9},{9,8},{10,11... | collective-permute-start | bytes 36872 | tf_op jit(solution)/shard_map/ppermute | solution.py:423
  8.5 0.0 collective-permute-done.rows_a_ref
  8.5 1.5 %collective-permute-start.1 = (f32[24,128]{1,0:T(8,128)S(1)}, f32[24,128]{1,0:T(8,128)S(1)}, u32[]{:S(2)}, u32[]{:S(2)}) collective-permute-start(f32[24,128]{1,0:T(8,128)S(1)} %collective-permute-done.rows_a_ref), channel_id=1, source_target_pairs={{0,16},{8,24},{16,0},{24,8},{1,17},{9,25},{17,1},{25,9},{2,18},{10... | collective-permute-start | bytes 36872 | tf_op jit(solution)/shard_map/ppermute | solution.py:419
  10.0 0.0 collective-permute-done.3.cols_b_ref
  10.0 0.0 collective-permute-done.2.cols_a_ref
  10.0 2.2 %collective-permute-done.1.rows_b_ref = f32[24,128]{1,0:T(8,128)S(1)} collective-permute-done((f32[24,128]{1,0:T(8,128)S(1)}, f32[24,128]{1,0:T(8,128)S(1)}, u32[]{:S(2)}, u32[]{:S(2)}) %collective-permute-start.1) | collective-permute-done | bytes 12320 | tf_op jit(solution)/shard_map/ppermute | solution.py:419
  12.2 0.0 copy-done.5
  12.2 0.0 copy-start.2
  12.2 0.0 copy-start.3
  12.2 0.0 copy-start
  12.2 0.0 copy-start.1
  12.3 0.8 %shard_map.114 = (f32[136,128]{1,0:T(8,128)S(1)}, s32[4,64]{1,0:T(4,128)S(1)}) custom-call(s32[1,64]{1,0:T(1,128)S(1)} %copy-done.6, f32[3,128,128]{2,1,0:T(8,128)S(1)} %get-tuple-element.14.fields_ref, f32[24,128]{1,0:T(8,128)S(1)} %get-tuple-element.15.edges_ref, f32[24,128]{1,0:T(8,128)S(1)} %collective-permute-done.rows_a_ref, ...), custom_call_target="tpu_custom_call" | custom-call | flops 4000000000 | bytes 30000000 | tf_op jit(solution)/shard_map/pallas_call | solution.py:424
  13.0 2.2 %collective-permute-start.6 = (f32[136,128]{1,0:T(8,128)S(1)}, f32[136,128]{1,0:T(8,128)S(1)}, u32[]{:S(2)}, u32[]{:S(2)}) collective-permute-start(f32[136,128]{1,0:T(8,128)S(1)} %get-tuple-element.17.block_ref.refs_0_), channel_id=1, source_target_pairs={{0,6},{1,7},{2,4},{3,5},{4,2},{5,3},{6,0},{7,1},{8,14},{9,15},{10,... | collective-permute-start | bytes 208904 | tf_op jit(solution)/shard_map/ppermute | solution.py:449
  15.2 0.9 %collective-permute-start.5 = (f32[136,128]{1,0:T(8,128)S(1)}, f32[136,128]{1,0:T(8,128)S(1)}, u32[]{:S(2)}, u32[]{:S(2)}) collective-permute-start(f32[136,128]{1,0:T(8,128)S(1)} %get-tuple-element.17.block_ref.refs_0_), channel_id=1, source_target_pairs={{0,4},{1,5},{2,6},{3,7},{4,0},{5,1},{6,2},{7,3},{8,12},{9,13},{10,... | collective-permute-start | bytes 208904 | tf_op jit(solution)/shard_map/ppermute | solution.py:449
  16.1 1.3 %collective-permute-start.4 = (f32[136,128]{1,0:T(8,128)S(1)}, f32[136,128]{1,0:T(8,128)S(1)}, u32[]{:S(2)}, u32[]{:S(2)}) collective-permute-start(f32[136,128]{1,0:T(8,128)S(1)} %get-tuple-element.17.block_ref.refs_0_), channel_id=1, source_target_pairs={{0,2},{1,3},{2,0},{3,1},{4,6},{5,7},{6,4},{7,5},{8,10},{9,11},{10,... | collective-permute-start | bytes 208904 | tf_op jit(solution)/shard_map/ppermute | solution.py:449
  17.5 0.0 collective-permute-start.7
  17.5 2.5 %collective-permute-done.6.refs_3_ = f32[136,128]{1,0:T(8,128)S(1)} collective-permute-done((f32[136,128]{1,0:T(8,128)S(1)}, f32[136,128]{1,0:T(8,128)S(1)}, u32[]{:S(2)}, u32[]{:S(2)}) %collective-permute-start.6) | collective-permute-done | bytes 69664 | tf_op jit(solution)/shard_map/ppermute | solution.py:449
  20.0 0.0 collective-permute-start.10
  20.0 2.2 %collective-permute-done.5.refs_2_ = f32[136,128]{1,0:T(8,128)S(1)} collective-permute-done((f32[136,128]{1,0:T(8,128)S(1)}, f32[136,128]{1,0:T(8,128)S(1)}, u32[]{:S(2)}, u32[]{:S(2)}) %collective-permute-start.5) | collective-permute-done | bytes 69664 | tf_op jit(solution)/shard_map/ppermute | solution.py:449
  22.1 0.0 collective-permute-start.9
  22.2 0.0 collective-permute-done.4.refs_1_
  22.2 0.5 %collective-permute-start.8 = (f32[136,128]{1,0:T(8,128)S(1)}, f32[136,128]{1,0:T(8,128)S(1)}, u32[]{:S(2)}, u32[]{:S(2)}) collective-permute-start(f32[136,128]{1,0:T(8,128)S(1)} %collective-permute-done.4.refs_1_), channel_id=1, source_target_pairs={{0,1},{1,0},{2,3},{3,2},{4,5},{5,4},{6,7},{7,6},{8,9},{9,8},{10,11... | collective-permute-start | bytes 208904 | tf_op jit(solution)/shard_map/ppermute | solution.py:449
  22.7 0.6 %shard_map.115 = (f32[128,128]{1,0:T(8,128)S(1)}, f32[64,256]{1,0:T(8,128)S(1)}, bf16[256,256]{1,0:T(8,128)(2,1)S(1)}, bf16[256,256]{1,0:T(8,128)(2,1)S(1)}, f32...) custom-call(f32[136,128]{1,0:T(8,128)S(1)} %get-tuple-element.17.block_ref.refs_0_, ...), custom_call_target="tpu_custom_call" | custom-call | tf_op jit(solution)/shard_map/pallas_call | solution.py:454
  23.3 0.0 collective-permute-done.7.refs_4_
  23.3 0.0 collective-permute-done.10.refs_7_
  23.3 0.1 collective-permute-done.9.refs_6_
  23.4 0.2 collective-permute-done.8.refs_5_
  23.6 0.0 copy-done.1
  23.6 2.4 %shard_map.116 = (f32[128,128]{1,0:T(8,128)}, f32[128,128]{1,0:T(8,128)}) custom-call(s32[4,64]{1,0:T(4,128)S(4)} %get-tuple-element.19.index_ref, s32[4,64]{1,0:T(4,128)S(4)} %get-tuple-element.20.rank_ref, f32[136,128]{1,0:T(8,128)S(1)} %get-tuple-element.17.block_ref.refs_0_, f32[136,128]{1,0:T(8,128)S(1)} %collective-permute-done.4.refs_1_, ...), custom_call_target="tpu_custom_call" | custom-call | tf_op jit(solution)/shard_map/pallas_call | solution.py:470
  (8 shorter events, 0.0 us)
Async XLA Ops:
  0.6 11.6 %copy-start.5 = (s32[1,64,4]{1,2,0:T(4,128)S(1)}, s32[1,64,4]{1,2,0:T(4,128)}, u32[]{:S(2)}) copy-start(s32[1,64,4]{1,2,0:T(4,128)} %param.16) | copy-start | bytes 3076
  0.6 11.6 %copy-start.4 = (s32[1,64,4]{1,2,0:T(4,128)S(1)}, s32[1,64,4]{1,2,0:T(4,128)}, u32[]{:S(2)}) copy-start(s32[1,64,4]{1,2,0:T(4,128)} %param.15) | copy-start | bytes 3076
  0.7 11.6 %copy-start.6 = (s32[1,64]{1,0:T(1,128)S(1)}, s32[1,64]{1,0:T(1,128)}, u32[]{:S(2)}) copy-start(s32[1,64]{1,0:T(1,128)} %flags_ref.1) | copy-start | bytes 772
  1.8 6.7 %collective-permute-start = (f32[24,128]{1,0:T(8,128)S(1)}, f32[24,128]{1,0:T(8,128)S(1)}, u32[]{:S(2)}, u32[]{:S(2)}) collective-permute-start(f32[24,128]{1,0:T(8,128)S(1)} %get-tuple-element.16), channel_id=1, source_target_pairs={{0,8},{8,0},{16,24},{24,16},{1,9},{9,1},{17,25},{25,17},{2,10},{10... | collective-permute-start | bytes 36872 | tf_op jit(solution)/shard_map/ppermute | solution.py:417
  4.8 5.2 %collective-permute-start.3 = (f32[24,128]{1,0:T(8,128)S(1)}, f32[24,128]{1,0:T(8,128)S(1)}, u32[]{:S(2)}, u32[]{:S(2)}) collective-permute-start(f32[24,128]{1,0:T(8,128)S(1)} %get-tuple-element.15.edges_ref), channel_id=1, source_target_pairs={{0,0},{1,2},{2,1},{3,4},{4,3},{5,6},{6,5},{7,7},{8,8},{9,10},{10,9... | collective-permute-start | bytes 36872 | tf_op jit(solution)/shard_map/ppermute | solution.py:422
  5.5 4.5 %collective-permute-start.2 = (f32[24,128]{1,0:T(8,128)S(1)}, f32[24,128]{1,0:T(8,128)S(1)}, u32[]{:S(2)}, u32[]{:S(2)}) collective-permute-start(f32[24,128]{1,0:T(8,128)S(1)} %get-tuple-element.15.edges_ref), channel_id=1, source_target_pairs={{0,1},{1,0},{2,3},{3,2},{4,5},{5,4},{6,7},{7,6},{8,9},{9,8},{10,11... | collective-permute-start | bytes 36872 | tf_op jit(solution)/shard_map/ppermute | solution.py:423
  8.5 3.7 %collective-permute-start.1 = (f32[24,128]{1,0:T(8,128)S(1)}, f32[24,128]{1,0:T(8,128)S(1)}, u32[]{:S(2)}, u32[]{:S(2)}) collective-permute-start(f32[24,128]{1,0:T(8,128)S(1)} %collective-permute-done.rows_a_ref), channel_id=1, source_target_pairs={{0,16},{8,24},{16,0},{24,8},{1,17},{9,25},{17,1},{25,9},{2,18},{10... | collective-permute-start | bytes 36872 | tf_op jit(solution)/shard_map/ppermute | solution.py:419
  12.2 10.5 %copy-start.2 = (f32[256,256]{1,0:T(8,128)S(1)}, f32[256,256]{1,0:T(8,128)}, u32[]{:S(2)}) copy-start(f32[256,256]{1,0:T(8,128)} %self_ref.1) | copy-start | bytes 786436
  12.2 10.4 %copy-start.3 = (s32[1,64,4]{1,2,0:T(4,128)S(1)}, s32[1,64,4]{1,2,0:T(4,128)}, u32[]{:S(2)}) copy-start(s32[1,64,4]{1,2,0:T(4,128)} %param.17) | copy-start | bytes 3076
  12.2 11.3 %copy-start = (f32[1,64,4,16,256]{4,3,2,1,0:T(8,128)S(1)}, f32[1,64,4,16,256]{4,3,2,1,0:T(8,128)}, u32[]{:S(2)}) copy-start(f32[1,64,4,16,256]{4,3,2,1,0:T(8,128)} %param.19) | copy-start | bytes 12582916
  12.2 11.3 %copy-start.1 = (f32[1,64,4,16,256]{4,3,2,1,0:T(8,128)S(1)}, f32[1,64,4,16,256]{4,3,2,1,0:T(8,128)}, u32[]{:S(2)}) copy-start(f32[1,64,4,16,256]{4,3,2,1,0:T(8,128)} %param.18) | copy-start | bytes 12582916
  13.0 6.9 %collective-permute-start.6 = (f32[136,128]{1,0:T(8,128)S(1)}, f32[136,128]{1,0:T(8,128)S(1)}, u32[]{:S(2)}, u32[]{:S(2)}) collective-permute-start(f32[136,128]{1,0:T(8,128)S(1)} %get-tuple-element.17.block_ref.refs_0_), channel_id=1, source_target_pairs={{0,6},{1,7},{2,4},{3,5},{4,2},{5,3},{6,0},{7,1},{8,14},{9,15},{10,... | collective-permute-start | bytes 208904 | tf_op jit(solution)/shard_map/ppermute | solution.py:449
  15.2 6.9 %collective-permute-start.5 = (f32[136,128]{1,0:T(8,128)S(1)}, f32[136,128]{1,0:T(8,128)S(1)}, u32[]{:S(2)}, u32[]{:S(2)}) collective-permute-start(f32[136,128]{1,0:T(8,128)S(1)} %get-tuple-element.17.block_ref.refs_0_), channel_id=1, source_target_pairs={{0,4},{1,5},{2,6},{3,7},{4,0},{5,1},{6,2},{7,3},{8,12},{9,13},{10,... | collective-permute-start | bytes 208904 | tf_op jit(solution)/shard_map/ppermute | solution.py:449
  16.1 6.0 %collective-permute-start.4 = (f32[136,128]{1,0:T(8,128)S(1)}, f32[136,128]{1,0:T(8,128)S(1)}, u32[]{:S(2)}, u32[]{:S(2)}) collective-permute-start(f32[136,128]{1,0:T(8,128)S(1)} %get-tuple-element.17.block_ref.refs_0_), channel_id=1, source_target_pairs={{0,2},{1,3},{2,0},{3,1},{4,6},{5,7},{6,4},{7,5},{8,10},{9,11},{10,... | collective-permute-start | bytes 208904 | tf_op jit(solution)/shard_map/ppermute | solution.py:449
  17.5 5.8 %collective-permute-start.7 = (f32[136,128]{1,0:T(8,128)S(1)}, f32[136,128]{1,0:T(8,128)S(1)}, u32[]{:S(2)}, u32[]{:S(2)}) collective-permute-start(f32[136,128]{1,0:T(8,128)S(1)} %get-tuple-element.17.block_ref.refs_0_), channel_id=1, source_target_pairs={{0,1},{1,0},{2,3},{3,2},{4,5},{5,4},{6,7},{7,6},{8,9},{9,8},{10,11... | collective-permute-start | bytes 208904 | tf_op jit(solution)/shard_map/ppermute | solution.py:449
  20.0 3.3 %collective-permute-start.10 = (f32[136,128]{1,0:T(8,128)S(1)}, f32[136,128]{1,0:T(8,128)S(1)}, u32[]{:S(2)}, u32[]{:S(2)}) collective-permute-start(f32[136,128]{1,0:T(8,128)S(1)} %collective-permute-done.6.refs_3_), channel_id=1, source_target_pairs={{0,1},{1,0},{2,3},{3,2},{4,5},{5,4},{6,7},{7,6},{8,9},{9,8},{10,11... | collective-permute-start | bytes 208904 | tf_op jit(solution)/shard_map/ppermute | solution.py:449
  22.1 1.3 %collective-permute-start.9 = (f32[136,128]{1,0:T(8,128)S(1)}, f32[136,128]{1,0:T(8,128)S(1)}, u32[]{:S(2)}, u32[]{:S(2)}) collective-permute-start(f32[136,128]{1,0:T(8,128)S(1)} %collective-permute-done.5.refs_2_), channel_id=1, source_target_pairs={{0,1},{1,0},{2,3},{3,2},{4,5},{5,4},{6,7},{7,6},{8,9},{9,8},{10,11... | collective-permute-start | bytes 208904 | tf_op jit(solution)/shard_map/ppermute | solution.py:449
  22.2 1.4 %collective-permute-start.8 = (f32[136,128]{1,0:T(8,128)S(1)}, f32[136,128]{1,0:T(8,128)S(1)}, u32[]{:S(2)}, u32[]{:S(2)}) collective-permute-start(f32[136,128]{1,0:T(8,128)S(1)} %collective-permute-done.4.refs_1_), channel_id=1, source_target_pairs={{0,1},{1,0},{2,3},{3,2},{4,5},{5,4},{6,7},{7,6},{8,9},{9,8},{10,11... | collective-permute-start | bytes 208904 | tf_op jit(solution)/shard_map/ppermute | solution.py:449
